TPU v7x, 512 devices: a whole 4x8x8 slice. The times are simulated.
512 devices in a mesh: gx: 32 (over y, x), gz: 16 (over z, core).
Axes of the slice: x: 4, y: 8, z: 8, core: 2. Of those that a mesh axis runs over, the one named last changes fastest.
Arguments:
- factor: float32 [3, 256, 4, 128, 256], P(None, 'gz', None, 'gx'), may hold values from -6 to 6
- gain: float32 [3, 256, 4, 128, 256], P(None, 'gz', None, 'gx'), may hold values from -6 to 6
- base_flow: float32 [256, 128, 256], P('gz', 'gx'), may hold values from 0.25 to 2
- shift_index: int32 [1], replicated, may hold values from 0 to 7
- sensor_cells: int32 [4, 4], replicated, may hold values from 0 to 255, as said below
Outputs:
- new_factor: float32 [3, 256, 4, 128, 256], P(None, 'gz', None, 'gx')
- new_gain: float32 [3, 256, 4, 128, 256], P(None, 'gz', None, 'gx')
- gram: float32 [4, 4], replicated
Inputs may be any that keep to these rules, and one draw needn't show every extreme that they name: `sensor_cells`: row i gives sensor i's velocity component (0 to 2), spanwise index (0 to 255), streamwise index (0 to 127) and wall-normal index (0 to 255); in every draw some sensor sits at spanwise index 255, some at streamwise index 127 and some at wall-normal index 255.
All inputs are finite; a program needn't handle non-finite values.
Results may differ from a plain program's by a relative error of at most 0.03.
Values sent between devices are 32-bit elements; how exact they have to be, the bound alone decides.
A program may use at most 64 MiB of HBM per device.

v0:
```python
import math

import jax
import jax.numpy as jnp
from jax import lax
from jax.sharding import PartitionSpec as P

SWEEPS = 3
POISSON = 4
SHIFTS = 8


viscosity = 0.4
shift_table = (0.6, 0.8, 1.0, 1.25, 1.6, 2.0, 2.5, 3.2)
chebyshev_weights = (1.0 / 1.9352976, 1.0 / 1.4752809, 1.0 / 0.8247191, 1.0 / 0.3647024)
highest = lax.Precision.HIGHEST


def padded_2(cells, sides, width, closed):
    for axis, dim in sides:
        count = lax.axis_size(axis)
        ends = count if closed else count - 1
        head = lax.slice_in_dim(cells, 0, width, axis=dim)
        tail = lax.slice_in_dim(cells, cells.shape[dim] - width, cells.shape[dim], axis=dim)
        cells = jnp.concatenate(
            [
                lax.ppermute(tail, axis, [(i, (i + 1) % count) for i in range(ends)]),
                cells,
                lax.ppermute(head, axis, [((i + 1) % count, i) for i in range(ends)]),
            ],
            axis=dim,
        )
    return cells


def around_sum(padded):
    summed = padded[:, 1:-1, :, 2:, 1:-1] + padded[:, 1:-1, :, :-2, 1:-1]
    summed = summed + padded[:, 1:-1, :, 1:-1, 2:] + padded[:, 1:-1, :, 1:-1, :-2]
    return summed + padded[:, 2:, :, 1:-1, 1:-1] + padded[:, :-2, :, 1:-1, 1:-1]


def shards(factor, gain, base_flow, shift_index, sensor_cells):
    components, span_cells, columns, stream_cells, normal_cells = factor.shape
    stream_start = lax.axis_index("gx") * stream_cells
    span_start = lax.axis_index("gz") * span_cells
    stream_total = stream_cells * lax.axis_size("gx")
    span_total = span_cells * lax.axis_size("gz")
    shift_values = jnp.asarray(shift_table, jnp.float32)
    shift_value = jnp.sum(jnp.where(jnp.arange(SHIFTS) == shift_index[0], shift_values, 0.0))
    base_field = base_flow[None, :, None, :, :]
    diagonal = shift_value + 6.0 * viscosity + base_field
    source = -factor

    def stream_inside(extent, margin):
        positions = stream_start - margin + jnp.arange(extent)
        return ((positions >= 0) & (positions < stream_total)).astype(jnp.float32)

    def extend(grid_field):
        padded = padded_2(grid_field, (("gx", 3), ("gz", 1)), 1, True)
        padded = padded * stream_inside(stream_cells + 2, 1)[None, None, None, :, None]
        return jnp.pad(padded, ((0, 0), (0, 0), (0, 0), (0, 0), (1, 1)))

    velocity = source / diagonal
    for sweep_index in range(SWEEPS):
        padded = extend(velocity)
        velocity = (
            source + viscosity * around_sum(padded) + base_field * padded[:, 1:-1, :, :-2, 1:-1]
        ) / diagonal
    padded = extend(velocity)
    divergence = 2.0 * (velocity[0] - padded[0, 1:-1, :, :-2, 1:-1])
    divergence = divergence + (velocity[1] - padded[1, 1:-1, :, 1:-1, :-2])
    divergence = divergence + (velocity[2] - padded[2, :-2, :, 1:-1, 1:-1])
    span_index = jnp.arange(span_total)
    products = span_index[:, None] * span_index[None, :] % span_total
    angles = 2.0 * math.pi * products.astype(jnp.float32) / span_total
    hartley_table = (jnp.cos(angles) + jnp.sin(angles)) / math.sqrt(span_total)

    def turn_modes(exchanged):
        turned = jnp.einsum("kz,zay->kay", hartley_table, exchanged, precision=highest)
        return lax.all_to_all(turned, "gz", split_axis=0, concat_axis=1, tiled=True)

    def transform(grid_field):
        flat = grid_field.reshape(span_cells, columns * stream_cells, normal_cells)
        result = turn_modes(lax.all_to_all(flat, "gz", split_axis=1, concat_axis=0, tiled=True))
        return result.reshape(span_cells, columns, stream_cells, normal_cells)

    modes_rhs = -transform(divergence)
    wave_index = span_start + jnp.arange(span_cells)
    wavenumber = 2.0 * math.pi * wave_index.astype(jnp.float32) / span_total
    mode_diagonal = (10.0 + (2.0 - 2.0 * jnp.cos(wavenumber)))[:, None, None, None]
    pressure = chebyshev_weights[0] * modes_rhs / mode_diagonal
    for sweep_level in range(1, POISSON):
        padded = padded_2(pressure, (("gx", 2),), 1, False)
        padded = jnp.pad(padded, ((0, 0), (0, 0), (0, 0), (1, 1)))
        beside_all = (
            4.0 * (padded[:, :, 2:, 1:-1] + padded[:, :, :-2, 1:-1])
            + padded[:, :, 1:-1, 2:]
            + padded[:, :, 1:-1, :-2]
        )
        pressure = (
            pressure
            + chebyshev_weights[sweep_level]
            * (modes_rhs - (mode_diagonal * pressure - beside_all))
            / mode_diagonal
        )
    pressure = transform(pressure)
    padded = extend(pressure[None])[0]
    gradient = jnp.stack(
        [
            2.0 * (padded[1:-1, :, 2:, 1:-1] - pressure),
            padded[1:-1, :, 1:-1, 2:] - pressure,
            padded[2:, :, 1:-1, 1:-1] - pressure,
        ]
    )
    solved = velocity - gradient
    span_ids = span_start + jnp.arange(span_cells)
    stream_ids = stream_start + jnp.arange(stream_cells)
    normal_ids = jnp.arange(normal_cells)
    located = span_ids[None, :, None, None] == sensor_cells[:, 1][:, None, None, None]
    located = located & (stream_ids[None, None, :, None] == sensor_cells[:, 2][:, None, None, None])
    located = located & (normal_ids[None, None, None, :] == sensor_cells[:, 3][:, None, None, None])
    picked = jnp.einsum("szxy,czjxy->scj", located.astype(jnp.float32), solved, precision=highest)
    chooser = (jnp.arange(3)[None, :] == sensor_cells[:, 0:1]).astype(jnp.float32)
    readout_local = jnp.sum(picked * chooser[:, :, None], axis=1)
    new_factor = factor + 2.0 * shift_value * solved
    gram_local = jnp.einsum("czixy,czjxy->ij", new_factor, new_factor, precision=highest)
    gram_total, readout = lax.psum((gram_local, readout_local), ("gx", "gz"))
    gram = gram_total / (3.0 * stream_total * normal_cells * span_total)
    new_gain = gain + 2.0 * shift_value * jnp.einsum(
        "czjxy,ij->czixy", solved, readout, precision=highest
    )
    return (new_factor, new_gain, gram)


def solution(mesh):
    placed = (
        P(None, "gz", None, "gx", None),
        P(None, "gz", None, "gx", None),
        P("gz", "gx", None),
        P(),
        P(),
    )
    return jax.shard_map(
        shards,
        mesh=mesh,
        in_specs=placed,
        out_specs=(P(None, "gz", None, "gx", None), P(None, "gz", None, "gx", None), P()),
        check_vma=False,
    )
```

profile of v0, /device:TPU:1, one launch (start us, length us, event | category | flops | bytes accessed | tf_op | source)
XLA Modules:
  0.0 330.8 jit_solution(6655700584625712328)
XLA Ops:
  1.3 1.3 fusion.75
  3.2 0.8 broadcast_add_fusion
  4.1 1.6 fusion.32
  5.8 3.9 %collective-permute-start = (f32[3,16,4,1,256]{4,1,3,2,0:T(8,128)S(1)}, f32[3,16,4,1,256]{4,1,3,2,0:T(8,128)S(1)}, u32[]{:S(2)}, u32[]{:S(2)}) collective-permute-start(f32[3,16,4,1,256]{4,1,3,2,0:T(8,128)S(1)} %get-tuple-element.37), channel_id=1, source_target_pairs={{0,16},{16,32},{32,48},{48,64},{64,80},{80,96},{96,112},{112,128},... | collective-permute-start | bytes 589832 | tf_op jit(solution)/shard_map/ppermute | solution.py:27
  9.7 6.1 %collective-permute-start.1 = (f32[3,16,4,1,256]{4,1,3,2,0:T(8,128)S(1)}, f32[3,16,4,1,256]{4,1,3,2,0:T(8,128)S(1)}, u32[]{:S(2)}, u32[]{:S(2)}) collective-permute-start(f32[3,16,4,1,256]{4,1,3,2,0:T(8,128)S(1)} %get-tuple-element.38), channel_id=1, source_target_pairs={{16,0},{32,16},{48,32},{64,48},{80,64},{96,80},{112,96},{128,112},... | collective-permute-start | bytes 589832 | tf_op jit(solution)/shard_map/ppermute | solution.py:29
  15.9 1.1 collective-permute-done
  16.9 1.5 collective-permute-done.1
  18.5 4.5 %collective-permute-start.2 = (f32[3,1,4,6,256]{4,1,3,2,0:T(1,128)S(1)}, f32[3,1,4,6,256]{4,1,3,2,0:T(1,128)S(1)}, u32[]{:S(2)}, u32[]{:S(2)}) collective-permute-start(f32[3,1,4,6,256]{4,1,3,2,0:T(1,128)S(1)} %get-tuple-element.26), channel_id=1, source_target_pairs={{0,1},{1,2},{2,3},{3,4},{4,5},{5,6},{6,7},{7,8},{8,9},{9,10},{10,1... | collective-permute-start | bytes 221192 | tf_op jit(solution)/shard_map/ppermute | solution.py:27
  23.0 2.1 collective-permute-start.3
  25.8 0.9 collective-permute-done.3
  27.2 1.2 fusion.11
  28.4 1.9 collective-permute-start.4
  30.4 7.4 %collective-permute-start.5 = (f32[3,16,4,1,256]{4,1,3,2,0:T(8,128)S(1)}, f32[3,16,4,1,256]{4,1,3,2,0:T(8,128)S(1)}, u32[]{:S(2)}, u32[]{:S(2)}) collective-permute-start(f32[3,16,4,1,256]{4,1,3,2,0:T(8,128)S(1)} %get-tuple-element.36), channel_id=1, source_target_pairs={{16,0},{32,16},{48,32},{64,48},{80,64},{96,80},{112,96},{128,112},... | collective-permute-start | bytes 589832 | tf_op jit(solution)/shard_map/ppermute | solution.py:29
  37.8 1.1 collective-permute-done.4
  38.9 1.5 collective-permute-done.5
  40.5 1.5 collective-permute-start.6
  42.0 3.3 %collective-permute-start.7 = (f32[3,1,4,6,256]{4,1,3,2,0:T(1,128)S(1)}, f32[3,1,4,6,256]{4,1,3,2,0:T(1,128)S(1)}, u32[]{:S(2)}, u32[]{:S(2)}) collective-permute-start(f32[3,1,4,6,256]{4,1,3,2,0:T(1,128)S(1)} %get-tuple-element.25), channel_id=1, source_target_pairs={{1,0},{2,1},{3,2},{4,3},{5,4},{6,5},{7,6},{8,7},{9,8},{10,9},{11,1... | collective-permute-start | bytes 221192 | tf_op jit(solution)/shard_map/ppermute | solution.py:29
  45.3 0.7 collective-permute-done.6
  46.6 1.2 fusion.19
  47.8 1.9 collective-permute-start.8
  49.8 7.4 %collective-permute-start.9 = (f32[3,16,4,1,256]{4,1,3,2,0:T(8,128)S(1)}, f32[3,16,4,1,256]{4,1,3,2,0:T(8,128)S(1)}, u32[]{:S(2)}, u32[]{:S(2)}) collective-permute-start(f32[3,16,4,1,256]{4,1,3,2,0:T(8,128)S(1)} %get-tuple-element.34), channel_id=1, source_target_pairs={{16,0},{32,16},{48,32},{64,48},{80,64},{96,80},{112,96},{128,112},... | collective-permute-start | bytes 589832 | tf_op jit(solution)/shard_map/ppermute | solution.py:29
  57.2 1.1 collective-permute-done.8
  58.3 1.5 collective-permute-done.9
  59.9 1.0 collective-permute-start.10
  60.9 4.5 %collective-permute-start.11 = (f32[3,1,4,6,256]{4,1,3,2,0:T(1,128)S(1)}, f32[3,1,4,6,256]{4,1,3,2,0:T(1,128)S(1)}, u32[]{:S(2)}, u32[]{:S(2)}) collective-permute-start(f32[3,1,4,6,256]{4,1,3,2,0:T(1,128)S(1)} %get-tuple-element.23), channel_id=1, source_target_pairs={{1,0},{2,1},{3,2},{4,3},{5,4},{6,5},{7,6},{8,7},{9,8},{10,9},{11,1... | collective-permute-start | bytes 221192 | tf_op jit(solution)/shard_map/ppermute | solution.py:29
  65.3 0.7 collective-permute-done.10
  66.7 1.2 fusion.27
  67.9 1.9 collective-permute-start.12
  69.8 7.4 %collective-permute-start.13 = (f32[3,16,4,1,256]{4,1,3,2,0:T(8,128)S(1)}, f32[3,16,4,1,256]{4,1,3,2,0:T(8,128)S(1)}, u32[]{:S(2)}, u32[]{:S(2)}) collective-permute-start(f32[3,16,4,1,256]{4,1,3,2,0:T(8,128)S(1)} %get-tuple-element.32), channel_id=1, source_target_pairs={{16,0},{32,16},{48,32},{64,48},{80,64},{96,80},{112,96},{128,112},... | collective-permute-start | bytes 589832 | tf_op jit(solution)/shard_map/ppermute | solution.py:29
  77.2 1.1 collective-permute-done.12
  78.4 1.5 collective-permute-done.13
  80.0 5.8 %collective-permute-start.15 = (f32[3,1,4,6,256]{4,1,3,2,0:T(1,128)S(1)}, f32[3,1,4,6,256]{4,1,3,2,0:T(1,128)S(1)}, u32[]{:S(2)}, u32[]{:S(2)}) collective-permute-start(f32[3,1,4,6,256]{4,1,3,2,0:T(1,128)S(1)} %get-tuple-element.21), channel_id=1, source_target_pairs={{1,0},{2,1},{3,2},{4,3},{5,4},{6,5},{7,6},{8,7},{9,8},{10,9},{11,1... | collective-permute-start | bytes 221192 | tf_op jit(solution)/shard_map/ppermute | solution.py:29
  85.8 0.7 collective-permute-done.14
  87.3 22.0 %all_to_all.54 = f32[16,16,256]{2,0,1:T(8,128)S(1)} all-to-all(f32[16,16,256]{2,0,1:T(8,128)S(1)} %bitcast.84), channel_id=1, replica_groups=mesh['gx'=32,'gz'=16] {'gz'}, dimensions={1} | all-to-all | bytes 524288 | tf_op jit(solution)/shard_map/all_to_all | solution.py:84
  109.3 1.7 convolution_bitcast_fusion.1
  111.0 1.0 copy.27
  112.0 3.4 %all-to-all-start.1 = ((f32[256,1,256]{2,1,0:T(1,128)}), f32[256,1,256]{2,1,0:T(1,128)S(1)}, u32[]{:S(2)}, u32[]{:S(2)}) async-start(f32[256,1,256]{2,1,0:T(1,128)} %copy.27), calls=%async_computation.1 | async-start | bytes 524288 | tf_op jit(solution)/shard_map/all_to_all | solution.py:80
  115.5 11.1 %all-to-all-done.1 = f32[256,1,256]{2,1,0:T(1,128)S(1)} async-done(((f32[256,1,256]{2,1,0:T(1,128)}), f32[256,1,256]{2,1,0:T(1,128)S(1)}, u32[]{:S(2)}, u32[]{:S(2)}) %all-to-all-start.1) | async-done | bytes 262176 | tf_op jit(solution)/shard_map/all_to_all | solution.py:80
  127.0 1.3 collective-permute-start.16
  128.3 4.0 %collective-permute-start.17 = (f32[16,4,1,256]{3,0,2,1:T(8,128)S(1)}, f32[16,4,1,256]{3,0,2,1:T(8,128)S(1)}, u32[]{:S(2)}, u32[]{:S(2)}) collective-permute-start(f32[16,4,1,256]{3,0,2,1:T(8,128)S(1)} %get-tuple-element.47), channel_id=1, source_target_pairs={{0,16},{16,32},{32,48},{48,64},{64,80},{80,96},{96,112},{112,128},... | collective-permute-start | bytes 196616 | tf_op jit(solution)/shard_map/ppermute | solution.py:27
  132.6 1.0 collective-permute-done.17
  134.0 1.3 collective-permute-start.18
  135.3 4.6 %collective-permute-start.19 = (f32[16,4,1,256]{3,0,2,1:T(8,128)S(1)}, f32[16,4,1,256]{3,0,2,1:T(8,128)S(1)}, u32[]{:S(2)}, u32[]{:S(2)}) collective-permute-start(f32[16,4,1,256]{3,0,2,1:T(8,128)S(1)} %get-tuple-element.45), channel_id=1, source_target_pairs={{0,16},{16,32},{32,48},{48,64},{64,80},{80,96},{96,112},{112,128},... | collective-permute-start | bytes 196616 | tf_op jit(solution)/shard_map/ppermute | solution.py:27
  139.9 1.3 collective-permute-done.19
  141.7 1.3 collective-permute-start.20
  143.0 4.3 %collective-permute-start.21 = (f32[16,4,1,256]{3,0,2,1:T(8,128)S(1)}, f32[16,4,1,256]{3,0,2,1:T(8,128)S(1)}, u32[]{:S(2)}, u32[]{:S(2)}) collective-permute-start(f32[16,4,1,256]{3,0,2,1:T(8,128)S(1)} %get-tuple-element.43), channel_id=1, source_target_pairs={{0,16},{16,32},{32,48},{48,64},{64,80},{80,96},{96,112},{112,128},... | collective-permute-start | bytes 196616 | tf_op jit(solution)/shard_map/ppermute | solution.py:27
  147.3 1.3 collective-permute-done.21
  148.8 0.9 fusion.47
  149.7 6.4 %all-to-all-start.2 = ((f32[16,16,256]{2,0,1:T(8,128)}), f32[16,16,256]{2,0,1:T(8,128)S(1)}, u32[]{:S(2)}, u32[]{:S(2)}) async-start(f32[16,16,256]{2,0,1:T(8,128)} %bitcast.8), calls=%async_computation.2 | async-start | bytes 524288 | tf_op jit(solution)/shard_map/all_to_all | solution.py:84
  156.4 11.4 %all-to-all-done.2 = f32[16,16,256]{2,0,1:T(8,128)S(1)} async-done(((f32[16,16,256]{2,0,1:T(8,128)}), f32[16,16,256]{2,0,1:T(8,128)S(1)}, u32[]{:S(2)}, u32[]{:S(2)}) %all-to-all-start.2) | async-done | bytes 262176 | tf_op jit(solution)/shard_map/all_to_all | solution.py:84
  167.8 1.7 convolution_bitcast_fusion
  169.6 1.0 copy.28
  170.5 3.6 %all-to-all-start.3 = ((f32[256,1,256]{2,1,0:T(1,128)}), f32[256,1,256]{2,1,0:T(1,128)S(1)}, u32[]{:S(2)}, u32[]{:S(2)}) async-start(f32[256,1,256]{2,1,0:T(1,128)} %copy.28), calls=%async_computation.3 | async-start | bytes 524288 | tf_op jit(solution)/shard_map/all_to_all | solution.py:80
  174.2 10.8 %all-to-all-done.3 = f32[256,1,256]{2,1,0:T(1,128)S(1)} async-done(((f32[256,1,256]{2,1,0:T(1,128)}), f32[256,1,256]{2,1,0:T(1,128)S(1)}, u32[]{:S(2)}, u32[]{:S(2)}) %all-to-all-start.3) | async-done | bytes 262176 | tf_op jit(solution)/shard_map/all_to_all | solution.py:80
  185.1 4.0 %collective-permute-start.22 = (f32[1,16,4,1,256]{4,1,3,2,0:T(8,128)S(1)}, f32[1,16,4,1,256]{4,1,3,2,0:T(8,128)S(1)}, u32[]{:S(2)}, u32[]{:S(2)}) collective-permute-start(f32[1,16,4,1,256]{4,1,3,2,0:T(8,128)S(1)} %get-tuple-element.41), channel_id=1, source_target_pairs={{0,16},{16,32},{32,48},{48,64},{64,80},{80,96},{96,112},{112,128},... | collective-permute-start | bytes 196616 | tf_op jit(solution)/shard_map/ppermute | solution.py:27
  189.1 6.7 %collective-permute-start.23 = (f32[1,16,4,1,256]{4,1,3,2,0:T(8,128)S(1)}, f32[1,16,4,1,256]{4,1,3,2,0:T(8,128)S(1)}, u32[]{:S(2)}, u32[]{:S(2)}) collective-permute-start(f32[1,16,4,1,256]{4,1,3,2,0:T(8,128)S(1)} %get-tuple-element.42), channel_id=1, source_target_pairs={{16,0},{32,16},{48,32},{64,48},{80,64},{96,80},{112,96},{128,112},... | collective-permute-start | bytes 196616 | tf_op jit(solution)/shard_map/ppermute | solution.py:29
  196.5 0.9 collective-permute-done.23
  198.9 2.3 collective-permute-done.25
  202.4 3.7 %convolution_bitcast_fusion.3 = f32[4,4]{1,0:T(4,128)S(1)} fusion(f32[3,16,4,4,256]{4,1,3,2,0:T(8,128)S(1)} %get-tuple-element.18), kind=kOutput, calls=%fused_computation.19 | convolution fusion | flops 9437184 | bytes 786496 | tf_op jit(solution)/shard_map/czixy,czjxy->ij/dot_general | solution.py:126
  206.2 4.4 %fusion.3 = f32[4,4]{1,0:T(4,128)S(1)} fusion(f32[3,16,4,4,256]{4,1,3,2,0:T(8,128)S(1)} %get-tuple-element.19, pred[4,256]{1,0:T(4,128)(4,1)S(1)} %iota_compare_fusion.2, pred[4,16,4]{0,1,2:T(8,128)(4,1)S(1)} %broadcast_and_fusion, f32[4,3]{0,1:T(4,128)S(1)} %fusion.74), kind=kOutput, calls=%fused_computation.18 | convolution fusion | flops 9502800 | bytes 787824 | tf_op jit(solution)/shard_map/szxy,czjxy->scj/dot_general | solution.py:122
  210.6 1.4 copy.36
  212.0 115.2 %all-reduce.8 = (f32[4,4]{1,0:T(4,128)S(1)}, f32[4,4]{1,0:T(4,128)S(1)}) all-reduce(f32[4,4]{1,0:T(4,128)S(1)} %fusion.3, f32[4,4]{1,0:T(4,128)S(1)} %convolution_bitcast_fusion.3), channel_id=1, replica_groups=mesh['gx'=32,'gz'=16] {'gx','gz'}, use_global_device_ids=true, to_apply=%region_2.3 | all-reduce | flops 32 | bytes 256 | tf_op jit(solution)/shard_map/psum | solution.py:127
  327.2 1.9 fusion.1
  329.1 1.1 copy.37
  (64 shorter events, 9.1 us)
Async XLA Ops:
  0.6 15.2 %copy-start.2 = (f32[16,4,256]{2,1,0:T(4,128)S(1)}, f32[16,4,256]{2,1,0:T(4,128)}, u32[]{:S(2)}) copy-start(f32[16,4,256]{2,1,0:T(4,128)} %param.8) | copy-start | bytes 196612
  5.8 11.2 %collective-permute-start = (f32[3,16,4,1,256]{4,1,3,2,0:T(8,128)S(1)}, f32[3,16,4,1,256]{4,1,3,2,0:T(8,128)S(1)}, u32[]{:S(2)}, u32[]{:S(2)}) collective-permute-start(f32[3,16,4,1,256]{4,1,3,2,0:T(8,128)S(1)} %get-tuple-element.37), channel_id=1, source_target_pairs={{0,16},{16,32},{32,48},{48,64},{64,80},{80,96},{96,112},{112,128},... | collective-permute-start | bytes 589832 | tf_op jit(solution)/shard_map/ppermute | solution.py:27
  9.7 8.7 %collective-permute-start.1 = (f32[3,16,4,1,256]{4,1,3,2,0:T(8,128)S(1)}, f32[3,16,4,1,256]{4,1,3,2,0:T(8,128)S(1)}, u32[]{:S(2)}, u32[]{:S(2)}) collective-permute-start(f32[3,16,4,1,256]{4,1,3,2,0:T(8,128)S(1)} %get-tuple-element.38), channel_id=1, source_target_pairs={{16,0},{32,16},{48,32},{64,48},{80,64},{96,80},{112,96},{128,112},... | collective-permute-start | bytes 589832 | tf_op jit(solution)/shard_map/ppermute | solution.py:29
  18.5 8.7 %copy-start = (f32[3,16,4,4,256]{4,3,2,1,0:T(4,128)S(1)}, f32[3,16,4,4,256]{4,3,2,1,0:T(4,128)}, u32[]{:S(2)}) copy-start(f32[3,16,4,4,256]{4,3,2,1,0:T(4,128)} %param.6) | copy-start | bytes 2359300
  18.5 7.3 %collective-permute-start.2 = (f32[3,1,4,6,256]{4,1,3,2,0:T(1,128)S(1)}, f32[3,1,4,6,256]{4,1,3,2,0:T(1,128)S(1)}, u32[]{:S(2)}, u32[]{:S(2)}) collective-permute-start(f32[3,1,4,6,256]{4,1,3,2,0:T(1,128)S(1)} %get-tuple-element.26), channel_id=1, source_target_pairs={{0,1},{1,2},{2,3},{3,4},{4,5},{5,6},{6,7},{7,8},{8,9},{9,10},{10,1... | collective-permute-start | bytes 221192 | tf_op jit(solution)/shard_map/ppermute | solution.py:27
  23.0 3.8 %collective-permute-start.3 = (f32[3,1,4,6,256]{4,1,3,2,0:T(1,128)S(1)}, f32[3,1,4,6,256]{4,1,3,2,0:T(1,128)S(1)}, u32[]{:S(2)}, u32[]{:S(2)}) collective-permute-start(f32[3,1,4,6,256]{4,1,3,2,0:T(1,128)S(1)} %get-tuple-element.27), channel_id=1, source_target_pairs={{1,0},{2,1},{3,2},{4,3},{5,4},{6,5},{7,6},{8,7},{9,8},{10,9},{11,1... | collective-permute-start | bytes 221192 | tf_op jit(solution)/shard_map/ppermute | solution.py:29
  28.4 10.5 %collective-permute-start.4 = (f32[3,16,4,1,256]{4,1,3,2,0:T(8,128)S(1)}, f32[3,16,4,1,256]{4,1,3,2,0:T(8,128)S(1)}, u32[]{:S(2)}, u32[]{:S(2)}) collective-permute-start(f32[3,16,4,1,256]{4,1,3,2,0:T(8,128)S(1)} %get-tuple-element.35), channel_id=1, source_target_pairs={{0,16},{16,32},{32,48},{48,64},{64,80},{80,96},{96,112},{112,128},... | collective-permute-start | bytes 589832 | tf_op jit(solution)/shard_map/ppermute | solution.py:27
  30.4 10.0 %collective-permute-start.5 = (f32[3,16,4,1,256]{4,1,3,2,0:T(8,128)S(1)}, f32[3,16,4,1,256]{4,1,3,2,0:T(8,128)S(1)}, u32[]{:S(2)}, u32[]{:S(2)}) collective-permute-start(f32[3,16,4,1,256]{4,1,3,2,0:T(8,128)S(1)} %get-tuple-element.36), channel_id=1, source_target_pairs={{16,0},{32,16},{48,32},{64,48},{80,64},{96,80},{112,96},{128,112},... | collective-permute-start | bytes 589832 | tf_op jit(solution)/shard_map/ppermute | solution.py:29
  40.5 5.5 %collective-permute-start.6 = (f32[3,1,4,6,256]{4,1,3,2,0:T(1,128)S(1)}, f32[3,1,4,6,256]{4,1,3,2,0:T(1,128)S(1)}, u32[]{:S(2)}, u32[]{:S(2)}) collective-permute-start(f32[3,1,4,6,256]{4,1,3,2,0:T(1,128)S(1)} %get-tuple-element.24), channel_id=1, source_target_pairs={{0,1},{1,2},{2,3},{3,4},{4,5},{5,6},{6,7},{7,8},{8,9},{9,10},{10,1... | collective-permute-start | bytes 221192 | tf_op jit(solution)/shard_map/ppermute | solution.py:27
  42.0 4.3 %collective-permute-start.7 = (f32[3,1,4,6,256]{4,1,3,2,0:T(1,128)S(1)}, f32[3,1,4,6,256]{4,1,3,2,0:T(1,128)S(1)}, u32[]{:S(2)}, u32[]{:S(2)}) collective-permute-start(f32[3,1,4,6,256]{4,1,3,2,0:T(1,128)S(1)} %get-tuple-element.25), channel_id=1, source_target_pairs={{1,0},{2,1},{3,2},{4,3},{5,4},{6,5},{7,6},{8,7},{9,8},{10,9},{11,1... | collective-permute-start | bytes 221192 | tf_op jit(solution)/shard_map/ppermute | solution.py:29
  47.8 10.5 %collective-permute-start.8 = (f32[3,16,4,1,256]{4,1,3,2,0:T(8,128)S(1)}, f32[3,16,4,1,256]{4,1,3,2,0:T(8,128)S(1)}, u32[]{:S(2)}, u32[]{:S(2)}) collective-permute-start(f32[3,16,4,1,256]{4,1,3,2,0:T(8,128)S(1)} %get-tuple-element.33), channel_id=1, source_target_pairs={{0,16},{16,32},{32,48},{48,64},{64,80},{80,96},{96,112},{112,128},... | collective-permute-start | bytes 589832 | tf_op jit(solution)/shard_map/ppermute | solution.py:27
  49.8 10.0 %collective-permute-start.9 = (f32[3,16,4,1,256]{4,1,3,2,0:T(8,128)S(1)}, f32[3,16,4,1,256]{4,1,3,2,0:T(8,128)S(1)}, u32[]{:S(2)}, u32[]{:S(2)}) collective-permute-start(f32[3,16,4,1,256]{4,1,3,2,0:T(8,128)S(1)} %get-tuple-element.34), channel_id=1, source_target_pairs={{16,0},{32,16},{48,32},{64,48},{80,64},{96,80},{112,96},{128,112},... | collective-permute-start | bytes 589832 | tf_op jit(solution)/shard_map/ppermute | solution.py:29
  59.9 6.2 %collective-permute-start.10 = (f32[3,1,4,6,256]{4,1,3,2,0:T(1,128)S(1)}, f32[3,1,4,6,256]{4,1,3,2,0:T(1,128)S(1)}, u32[]{:S(2)}, u32[]{:S(2)}) collective-permute-start(f32[3,1,4,6,256]{4,1,3,2,0:T(1,128)S(1)} %get-tuple-element.22), channel_id=1, source_target_pairs={{0,1},{1,2},{2,3},{3,4},{4,5},{5,6},{6,7},{7,8},{8,9},{9,10},{10,1... | collective-permute-start | bytes 221192 | tf_op jit(solution)/shard_map/ppermute | solution.py:27
  60.9 5.4 %collective-permute-start.11 = (f32[3,1,4,6,256]{4,1,3,2,0:T(1,128)S(1)}, f32[3,1,4,6,256]{4,1,3,2,0:T(1,128)S(1)}, u32[]{:S(2)}, u32[]{:S(2)}) collective-permute-start(f32[3,1,4,6,256]{4,1,3,2,0:T(1,128)S(1)} %get-tuple-element.23), channel_id=1, source_target_pairs={{1,0},{2,1},{3,2},{4,3},{5,4},{6,5},{7,6},{8,7},{9,8},{10,9},{11,1... | collective-permute-start | bytes 221192 | tf_op jit(solution)/shard_map/ppermute | solution.py:29
  67.9 10.5 %collective-permute-start.12 = (f32[3,16,4,1,256]{4,1,3,2,0:T(8,128)S(1)}, f32[3,16,4,1,256]{4,1,3,2,0:T(8,128)S(1)}, u32[]{:S(2)}, u32[]{:S(2)}) collective-permute-start(f32[3,16,4,1,256]{4,1,3,2,0:T(8,128)S(1)} %get-tuple-element.31), channel_id=1, source_target_pairs={{0,16},{16,32},{32,48},{48,64},{64,80},{80,96},{96,112},{112,128},... | collective-permute-start | bytes 589832 | tf_op jit(solution)/shard_map/ppermute | solution.py:27
  69.8 10.0 %collective-permute-start.13 = (f32[3,16,4,1,256]{4,1,3,2,0:T(8,128)S(1)}, f32[3,16,4,1,256]{4,1,3,2,0:T(8,128)S(1)}, u32[]{:S(2)}, u32[]{:S(2)}) collective-permute-start(f32[3,16,4,1,256]{4,1,3,2,0:T(8,128)S(1)} %get-tuple-element.32), channel_id=1, source_target_pairs={{16,0},{32,16},{48,32},{64,48},{80,64},{96,80},{112,96},{128,112},... | collective-permute-start | bytes 589832 | tf_op jit(solution)/shard_map/ppermute | solution.py:29
  79.9 6.6 %collective-permute-start.14 = (f32[3,1,4,6,256]{4,1,3,2,0:T(1,128)S(1)}, f32[3,1,4,6,256]{4,1,3,2,0:T(1,128)S(1)}, u32[]{:S(2)}, u32[]{:S(2)}) collective-permute-start(f32[3,1,4,6,256]{4,1,3,2,0:T(1,128)S(1)} %get-tuple-element.20), channel_id=1, source_target_pairs={{0,1},{1,2},{2,3},{3,4},{4,5},{5,6},{6,7},{7,8},{8,9},{9,10},{10,1... | collective-permute-start | bytes 221192 | tf_op jit(solution)/shard_map/ppermute | solution.py:27
  80.0 6.7 %collective-permute-start.15 = (f32[3,1,4,6,256]{4,1,3,2,0:T(1,128)S(1)}, f32[3,1,4,6,256]{4,1,3,2,0:T(1,128)S(1)}, u32[]{:S(2)}, u32[]{:S(2)}) collective-permute-start(f32[3,1,4,6,256]{4,1,3,2,0:T(1,128)S(1)} %get-tuple-element.21), channel_id=1, source_target_pairs={{1,0},{2,1},{3,2},{4,3},{5,4},{6,5},{7,6},{8,7},{9,8},{10,9},{11,1... | collective-permute-start | bytes 221192 | tf_op jit(solution)/shard_map/ppermute | solution.py:29
  112.0 14.6 %all-to-all-start.1 = ((f32[256,1,256]{2,1,0:T(1,128)}), f32[256,1,256]{2,1,0:T(1,128)S(1)}, u32[]{:S(2)}, u32[]{:S(2)}) async-start(f32[256,1,256]{2,1,0:T(1,128)} %copy.27), calls=%async_computation.1 | async-start | bytes 524288 | tf_op jit(solution)/shard_map/all_to_all | solution.py:80
  127.0 5.6 %collective-permute-start.16 = (f32[16,4,1,256]{3,0,2,1:T(8,128)S(1)}, f32[16,4,1,256]{3,0,2,1:T(8,128)S(1)}, u32[]{:S(2)}, u32[]{:S(2)}) collective-permute-start(f32[16,4,1,256]{3,0,2,1:T(8,128)S(1)} %get-tuple-element.48), channel_id=1, source_target_pairs={{16,0},{32,16},{48,32},{64,48},{80,64},{96,80},{112,96},{128,112},... | collective-permute-start | bytes 196616 | tf_op jit(solution)/shard_map/ppermute | solution.py:29
  128.3 5.3 %collective-permute-start.17 = (f32[16,4,1,256]{3,0,2,1:T(8,128)S(1)}, f32[16,4,1,256]{3,0,2,1:T(8,128)S(1)}, u32[]{:S(2)}, u32[]{:S(2)}) collective-permute-start(f32[16,4,1,256]{3,0,2,1:T(8,128)S(1)} %get-tuple-element.47), channel_id=1, source_target_pairs={{0,16},{16,32},{32,48},{48,64},{64,80},{80,96},{96,112},{112,128},... | collective-permute-start | bytes 196616 | tf_op jit(solution)/shard_map/ppermute | solution.py:27
  134.0 6.0 %collective-permute-start.18 = (f32[16,4,1,256]{3,0,2,1:T(8,128)S(1)}, f32[16,4,1,256]{3,0,2,1:T(8,128)S(1)}, u32[]{:S(2)}, u32[]{:S(2)}) collective-permute-start(f32[16,4,1,256]{3,0,2,1:T(8,128)S(1)} %get-tuple-element.46), channel_id=1, source_target_pairs={{16,0},{32,16},{48,32},{64,48},{80,64},{96,80},{112,96},{128,112},... | collective-permute-start | bytes 196616 | tf_op jit(solution)/shard_map/ppermute | solution.py:29
  135.3 6.0 %collective-permute-start.19 = (f32[16,4,1,256]{3,0,2,1:T(8,128)S(1)}, f32[16,4,1,256]{3,0,2,1:T(8,128)S(1)}, u32[]{:S(2)}, u32[]{:S(2)}) collective-permute-start(f32[16,4,1,256]{3,0,2,1:T(8,128)S(1)} %get-tuple-element.45), channel_id=1, source_target_pairs={{0,16},{16,32},{32,48},{48,64},{64,80},{80,96},{96,112},{112,128},... | collective-permute-start | bytes 196616 | tf_op jit(solution)/shard_map/ppermute | solution.py:27
  141.7 14.5 %copy-start.3 = (s32[4,4]{1,0:T(4,128)S(1)}, s32[4,4]{1,0:T(4,128)}, u32[]{:S(2)}) copy-start(s32[4,4]{1,0:T(4,128)} %param.10) | copy-start | bytes 196
  141.7 5.6 %collective-permute-start.20 = (f32[16,4,1,256]{3,0,2,1:T(8,128)S(1)}, f32[16,4,1,256]{3,0,2,1:T(8,128)S(1)}, u32[]{:S(2)}, u32[]{:S(2)}) collective-permute-start(f32[16,4,1,256]{3,0,2,1:T(8,128)S(1)} %get-tuple-element.44), channel_id=1, source_target_pairs={{16,0},{32,16},{48,32},{64,48},{80,64},{96,80},{112,96},{128,112},... | collective-permute-start | bytes 196616 | tf_op jit(solution)/shard_map/ppermute | solution.py:29
  143.0 5.6 %collective-permute-start.21 = (f32[16,4,1,256]{3,0,2,1:T(8,128)S(1)}, f32[16,4,1,256]{3,0,2,1:T(8,128)S(1)}, u32[]{:S(2)}, u32[]{:S(2)}) collective-permute-start(f32[16,4,1,256]{3,0,2,1:T(8,128)S(1)} %get-tuple-element.43), channel_id=1, source_target_pairs={{0,16},{16,32},{32,48},{48,64},{64,80},{80,96},{96,112},{112,128},... | collective-permute-start | bytes 196616 | tf_op jit(solution)/shard_map/ppermute | solution.py:27
  149.7 18.1 %all-to-all-start.2 = ((f32[16,16,256]{2,0,1:T(8,128)}), f32[16,16,256]{2,0,1:T(8,128)S(1)}, u32[]{:S(2)}, u32[]{:S(2)}) async-start(f32[16,16,256]{2,0,1:T(8,128)} %bitcast.8), calls=%async_computation.2 | async-start | bytes 524288 | tf_op jit(solution)/shard_map/all_to_all | solution.py:84
  170.5 14.5 %all-to-all-start.3 = ((f32[256,1,256]{2,1,0:T(1,128)}), f32[256,1,256]{2,1,0:T(1,128)S(1)}, u32[]{:S(2)}, u32[]{:S(2)}) async-start(f32[256,1,256]{2,1,0:T(1,128)} %copy.28), calls=%async_computation.3 | async-start | bytes 524288 | tf_op jit(solution)/shard_map/all_to_all | solution.py:80
  185.1 11.3 %collective-permute-start.22 = (f32[1,16,4,1,256]{4,1,3,2,0:T(8,128)S(1)}, f32[1,16,4,1,256]{4,1,3,2,0:T(8,128)S(1)}, u32[]{:S(2)}, u32[]{:S(2)}) collective-permute-start(f32[1,16,4,1,256]{4,1,3,2,0:T(8,128)S(1)} %get-tuple-element.41), channel_id=1, source_target_pairs={{0,16},{16,32},{32,48},{48,64},{64,80},{80,96},{96,112},{112,128},... | collective-permute-start | bytes 196616 | tf_op jit(solution)/shard_map/ppermute | solution.py:27
  189.1 8.3 %collective-permute-start.23 = (f32[1,16,4,1,256]{4,1,3,2,0:T(8,128)S(1)}, f32[1,16,4,1,256]{4,1,3,2,0:T(8,128)S(1)}, u32[]{:S(2)}, u32[]{:S(2)}) collective-permute-start(f32[1,16,4,1,256]{4,1,3,2,0:T(8,128)S(1)} %get-tuple-element.42), channel_id=1, source_target_pairs={{16,0},{32,16},{48,32},{64,48},{80,64},{96,80},{112,96},{128,112},... | collective-permute-start | bytes 196616 | tf_op jit(solution)/shard_map/ppermute | solution.py:29
  197.4 1.4 collective-permute-start.24
  197.9 3.3 collective-permute-start.25
  202.4 124.8 %copy-start.1 = (f32[3,16,4,4,256]{4,3,2,1,0:T(4,128)S(1)}, f32[3,16,4,4,256]{4,3,2,1,0:T(4,128)}, u32[]{:S(2)}) copy-start(f32[3,16,4,4,256]{4,3,2,1,0:T(4,128)} %param.7) | copy-start | bytes 2359300
where the time goes:
time: 332 us; the launch traced here: 331 us
  blocking collectives  137 us (41%)
  starting transfers between devices  102 us (31%)
  waiting for transfers between devices  55.9 us (17%)
  other arithmetic  13.5 us (4%)
  matrix products  13.4 us (4%)
  local copies, waits for them, and re-layouts  5.2 us (2%)
    psum x1, blocking collectives, shards(): gram_total, readout = lax.psum((gram_local, readout_local), ('gx', 'gz'))  115 us
    ppermute x13, starting transfers between devices, padded_2(): lax.ppermute(head, axis, [((i + 1) % count, i) for i in range(ends)])  54.9 us
    ppermute x13, starting transfers between devices, padded_2(): lax.ppermute(tail, axis, [(i, (i + 1) % count) for i in range(ends)])  34.1 us
    all_to_all x1, blocking collectives, transform(): lax.all_to_all(flat, 'gz', split_axis=1, concat_axis=0, tiled=True)  22 us
    all_to_all x2, waiting for transfers between devices, turn_modes(): return lax.all_to_all(turned, 'gz', split_axis=0, concat_axis=1, tiled=True)  21.9 us
    ppermute x13, waiting for transfers between devices, padded_2(): lax.ppermute(tail, axis, [(i, (i + 1) % count) for i in range(ends)])  11.6 us
    all_to_all x1, waiting for transfers between devices, transform(): lax.all_to_all(flat, 'gz', split_axis=1, concat_axis=0, tiled=True)  11.4 us
    ppermute x13, waiting for transfers between devices, padded_2(): lax.ppermute(head, axis, [((i + 1) % count, i) for i in range(ends)])  10.9 us
  transfers between devices with their start and end apart: 29, of which 26 were waited for; matrix products, arithmetic and copies ran while one was open for 0% of the time, Pallas kernels for 0%

commit v1 on v0

--- a/solution.py
+++ b/solution.py
@@ -1,8 +1,11 @@
+import functools
 import math
 
 import jax
 import jax.numpy as jnp
 from jax import lax
+from jax.experimental import pallas as pl
+from jax.experimental.pallas import tpu as pltpu
 from jax.sharding import PartitionSpec as P
 
 SWEEPS = 3
@@ -37,6 +40,84 @@
     summed = padded[:, 1:-1, :, 2:, 1:-1] + padded[:, 1:-1, :, :-2, 1:-1]
     summed = summed + padded[:, 1:-1, :, 1:-1, 2:] + padded[:, 1:-1, :, 1:-1, :-2]
     return summed + padded[:, 2:, :, 1:-1, 1:-1] + padded[:, :-2, :, 1:-1, 1:-1]
+
+
+def sum_kernel(sizes, tile_ref, out_ref, slots_z, slots_x, slots_y, mid, sends, recvs):
+    count_z, count_x, count_y = sizes
+    gx, gz = lax.axis_index("gx"), lax.axis_index("gz")
+    here_x, here_y = gx % count_x, gx // count_x
+
+    def partner(stage, offset):
+        if stage == 0:
+            return (gx, (gz + offset) % count_z)
+        if stage == 1:
+            return (here_y * count_x + (here_x + offset) % count_x, gz)
+        return ((here_y + offset) % count_y * count_x + here_x, gz)
+
+    counts = (count_z, count_x, count_y)
+    barrier = pltpu.get_barrier_semaphore()
+    for stage in range(3):
+        def greet(offset, carry, stage=stage):
+            pl.semaphore_signal(
+                barrier, inc=1, device_id=partner(stage, offset), device_id_type=pl.DeviceIdType.MESH
+            )
+            return carry
+
+        lax.fori_loop(1, counts[stage], greet, 0)
+    pl.semaphore_wait(barrier, sum(counts) - 3)
+    places = (gz, here_x, here_y)
+    bases = (0, count_z, count_z + count_x)
+    source = tile_ref
+    for stage, slots in enumerate((slots_z, slots_x, slots_y)):
+        base = bases[stage]
+
+        def copy(offset, stage=stage, slots=slots, base=base, source=source):
+            return pltpu.make_async_remote_copy(
+                src_ref=source,
+                dst_ref=slots.at[places[stage]],
+                send_sem=sends.at[base + offset],
+                recv_sem=recvs.at[base + offset],
+                device_id=partner(stage, offset),
+                device_id_type=pl.DeviceIdType.MESH,
+            )
+
+        def start(offset, carry, copy=copy):
+            copy(offset).start()
+            return carry
+
+        def finish(offset, carry, copy=copy):
+            copy(offset).wait()
+            return carry
+
+        lax.fori_loop(1, counts[stage], start, 0)
+        slots[places[stage]] = source[...]
+        lax.fori_loop(1, counts[stage], finish, 0)
+        total = slots[0]
+        for place in range(1, counts[stage]):
+            total = total + slots[place]
+        if stage < 2:
+            mid[stage] = total
+            source = mid.at[stage]
+        else:
+            out_ref[...] = total
+
+
+def sum_all(tile, sizes):
+    count = sum(sizes)
+    return pl.pallas_call(
+        functools.partial(sum_kernel, sizes),
+        out_shape=jax.ShapeDtypeStruct((8, 128), jnp.float32),
+        in_specs=[pl.BlockSpec(memory_space=pltpu.VMEM)],
+        out_specs=pl.BlockSpec(memory_space=pltpu.VMEM),
+        scratch_shapes=[pltpu.VMEM((size, 8, 128), jnp.float32) for size in sizes]
+        + [
+            pltpu.VMEM((2, 8, 128), jnp.float32),
+            pltpu.SemaphoreType.DMA((count,)),
+            pltpu.SemaphoreType.DMA((count,)),
+        ],
+        compiler_params=pltpu.CompilerParams(collective_id=0, has_side_effects=True),
+        name="sum_all",
+    )(tile)
 
 
 def shards(factor, gain, base_flow, shift_index, sensor_cells):
@@ -124,7 +205,10 @@
     readout_local = jnp.sum(picked * chooser[:, :, None], axis=1)
     new_factor = factor + 2.0 * shift_value * solved
     gram_local = jnp.einsum("czixy,czjxy->ij", new_factor, new_factor, precision=highest)
-    gram_total, readout = lax.psum((gram_local, readout_local), ("gx", "gz"))
+    tile = jnp.pad(jnp.concatenate([gram_local, readout_local]), ((0, 0), (0, 124)))
+    count_gx = lax.axis_size("gx")
+    tile = sum_all(tile, (lax.axis_size("gz"), 4, count_gx // 4))
+    gram_total, readout = tile[:4, :4], tile[4:8, :4]
     gram = gram_total / (3.0 * stream_total * normal_cells * span_total)
     new_gain = gain + 2.0 * shift_value * jnp.einsum(
         "czjxy,ij->czixy", solved, readout, precision=highest

time: 332 us -> 255 us (0.77)
  blocking collectives: 137 us -> 22 us
  Pallas kernels: 0 us -> 36.6 us
    psum x1 -> x0, blocking collectives: 115 us -> none  [shards(): gram_total, readout = lax.psum((gram_local, readout_local), ('gx', 'gz'))]
    pallas_call x0 -> x1, Pallas kernels: none -> 36.6 us  [sum_all(): pl.pallas_call(functools.partial(sum_kernel, sizes), out_shape=jax.ShapeD...]
where the time goes in v1:
time: 255 us; the launch traced here: 254 us
  starting transfers between devices  102 us (40%)
  waiting for transfers between devices  55.9 us (22%)
  Pallas kernels  36.6 us (14%)
  blocking collectives  22 us (9%)
  other arithmetic  14.8 us (6%)
  matrix products  14.1 us (6%)
  local copies, waits for them, and re-layouts  5.19 us (2%)
  between operations  3.13 us (1%)
    ppermute x13, starting transfers between devices, padded_2(): lax.ppermute(head, axis, [((i + 1) % count, i) for i in range(ends)])  54.9 us
    pallas_call x1, Pallas kernels, sum_all(): pl.pallas_call(functools.partial(sum_kernel, sizes), out_shape=jax.ShapeD...  36.6 us
    ppermute x13, starting transfers between devices, padded_2(): lax.ppermute(tail, axis, [(i, (i + 1) % count) for i in range(ends)])  34.1 us
    all_to_all x1, blocking collectives, transform(): lax.all_to_all(flat, 'gz', split_axis=1, concat_axis=0, tiled=True)  22 us
    all_to_all x2, waiting for transfers between devices, turn_modes(): return lax.all_to_all(turned, 'gz', split_axis=0, concat_axis=1, tiled=True)  21.9 us
    ppermute x13, waiting for transfers between devices, padded_2(): lax.ppermute(tail, axis, [(i, (i + 1) % count) for i in range(ends)])  11.6 us
    all_to_all x1, waiting for transfers between devices, transform(): lax.all_to_all(flat, 'gz', split_axis=1, concat_axis=0, tiled=True)  11.4 us
    ppermute x13, waiting for transfers between devices, padded_2(): lax.ppermute(head, axis, [((i + 1) % count, i) for i in range(ends)])  11 us
  transfers between devices with their start and end apart: 29, of which 26 were waited for; matrix products, arithmetic and copies ran while one was open for 0% of the time, Pallas kernels for 0%

profile of v1, /device:TPU:1, one launch (start us, length us, event | category | flops | bytes accessed | tf_op | source)
XLA Modules:
  0.0 254.1 jit_solution(4200552151770005728)
XLA Ops:
  1.3 1.3 fusion.76
  3.2 0.8 broadcast_add_fusion
  4.1 1.6 fusion.32
  5.8 3.9 %collective-permute-start = (f32[3,16,4,1,256]{4,1,3,2,0:T(8,128)S(1)}, f32[3,16,4,1,256]{4,1,3,2,0:T(8,128)S(1)}, u32[]{:S(2)}, u32[]{:S(2)}) collective-permute-start(f32[3,16,4,1,256]{4,1,3,2,0:T(8,128)S(1)} %get-tuple-element.35), channel_id=1, source_target_pairs={{0,16},{16,32},{32,48},{48,64},{64,80},{80,96},{96,112},{112,128},... | collective-permute-start | bytes 589832 | tf_op jit(solution)/shard_map/ppermute | solution.py:30
  9.7 6.1 %collective-permute-start.1 = (f32[3,16,4,1,256]{4,1,3,2,0:T(8,128)S(1)}, f32[3,16,4,1,256]{4,1,3,2,0:T(8,128)S(1)}, u32[]{:S(2)}, u32[]{:S(2)}) collective-permute-start(f32[3,16,4,1,256]{4,1,3,2,0:T(8,128)S(1)} %get-tuple-element.36), channel_id=1, source_target_pairs={{16,0},{32,16},{48,32},{64,48},{80,64},{96,80},{112,96},{128,112},... | collective-permute-start | bytes 589832 | tf_op jit(solution)/shard_map/ppermute | solution.py:32
  15.9 1.1 collective-permute-done
  16.9 1.5 collective-permute-done.1
  18.5 4.5 %collective-permute-start.2 = (f32[3,1,4,6,256]{4,1,3,2,0:T(1,128)S(1)}, f32[3,1,4,6,256]{4,1,3,2,0:T(1,128)S(1)}, u32[]{:S(2)}, u32[]{:S(2)}) collective-permute-start(f32[3,1,4,6,256]{4,1,3,2,0:T(1,128)S(1)} %get-tuple-element.24), channel_id=1, source_target_pairs={{0,1},{1,2},{2,3},{3,4},{4,5},{5,6},{6,7},{7,8},{8,9},{9,10},{10,1... | collective-permute-start | bytes 221192 | tf_op jit(solution)/shard_map/ppermute | solution.py:30
  23.0 2.1 collective-permute-start.3
  25.8 0.9 collective-permute-done.3
  27.2 1.2 fusion.11
  28.4 1.9 collective-permute-start.4
  30.4 7.4 %collective-permute-start.5 = (f32[3,16,4,1,256]{4,1,3,2,0:T(8,128)S(1)}, f32[3,16,4,1,256]{4,1,3,2,0:T(8,128)S(1)}, u32[]{:S(2)}, u32[]{:S(2)}) collective-permute-start(f32[3,16,4,1,256]{4,1,3,2,0:T(8,128)S(1)} %get-tuple-element.34), channel_id=1, source_target_pairs={{16,0},{32,16},{48,32},{64,48},{80,64},{96,80},{112,96},{128,112},... | collective-permute-start | bytes 589832 | tf_op jit(solution)/shard_map/ppermute | solution.py:32
  37.8 1.1 collective-permute-done.4
  38.9 1.5 collective-permute-done.5
  40.5 1.5 collective-permute-start.6
  42.0 3.3 %collective-permute-start.7 = (f32[3,1,4,6,256]{4,1,3,2,0:T(1,128)S(1)}, f32[3,1,4,6,256]{4,1,3,2,0:T(1,128)S(1)}, u32[]{:S(2)}, u32[]{:S(2)}) collective-permute-start(f32[3,1,4,6,256]{4,1,3,2,0:T(1,128)S(1)} %get-tuple-element.23), channel_id=1, source_target_pairs={{1,0},{2,1},{3,2},{4,3},{5,4},{6,5},{7,6},{8,7},{9,8},{10,9},{11,1... | collective-permute-start | bytes 221192 | tf_op jit(solution)/shard_map/ppermute | solution.py:32
  45.3 0.7 collective-permute-done.6
  46.6 1.2 fusion.19
  47.8 1.9 collective-permute-start.8
  49.8 7.4 %collective-permute-start.9 = (f32[3,16,4,1,256]{4,1,3,2,0:T(8,128)S(1)}, f32[3,16,4,1,256]{4,1,3,2,0:T(8,128)S(1)}, u32[]{:S(2)}, u32[]{:S(2)}) collective-permute-start(f32[3,16,4,1,256]{4,1,3,2,0:T(8,128)S(1)} %get-tuple-element.32), channel_id=1, source_target_pairs={{16,0},{32,16},{48,32},{64,48},{80,64},{96,80},{112,96},{128,112},... | collective-permute-start | bytes 589832 | tf_op jit(solution)/shard_map/ppermute | solution.py:32
  57.2 1.1 collective-permute-done.8
  58.3 1.5 collective-permute-done.9
  59.9 1.0 collective-permute-start.10
  60.9 4.5 %collective-permute-start.11 = (f32[3,1,4,6,256]{4,1,3,2,0:T(1,128)S(1)}, f32[3,1,4,6,256]{4,1,3,2,0:T(1,128)S(1)}, u32[]{:S(2)}, u32[]{:S(2)}) collective-permute-start(f32[3,1,4,6,256]{4,1,3,2,0:T(1,128)S(1)} %get-tuple-element.21), channel_id=1, source_target_pairs={{1,0},{2,1},{3,2},{4,3},{5,4},{6,5},{7,6},{8,7},{9,8},{10,9},{11,1... | collective-permute-start | bytes 221192 | tf_op jit(solution)/shard_map/ppermute | solution.py:32
  65.3 0.7 collective-permute-done.10
  66.7 1.2 fusion.27
  67.9 1.9 collective-permute-start.12
  69.8 7.4 %collective-permute-start.13 = (f32[3,16,4,1,256]{4,1,3,2,0:T(8,128)S(1)}, f32[3,16,4,1,256]{4,1,3,2,0:T(8,128)S(1)}, u32[]{:S(2)}, u32[]{:S(2)}) collective-permute-start(f32[3,16,4,1,256]{4,1,3,2,0:T(8,128)S(1)} %get-tuple-element.30), channel_id=1, source_target_pairs={{16,0},{32,16},{48,32},{64,48},{80,64},{96,80},{112,96},{128,112},... | collective-permute-start | bytes 589832 | tf_op jit(solution)/shard_map/ppermute | solution.py:32
  77.2 1.1 collective-permute-done.12
  78.4 1.5 collective-permute-done.13
  80.0 5.8 %collective-permute-start.15 = (f32[3,1,4,6,256]{4,1,3,2,0:T(1,128)S(1)}, f32[3,1,4,6,256]{4,1,3,2,0:T(1,128)S(1)}, u32[]{:S(2)}, u32[]{:S(2)}) collective-permute-start(f32[3,1,4,6,256]{4,1,3,2,0:T(1,128)S(1)} %get-tuple-element.19), channel_id=1, source_target_pairs={{1,0},{2,1},{3,2},{4,3},{5,4},{6,5},{7,6},{8,7},{9,8},{10,9},{11,1... | collective-permute-start | bytes 221192 | tf_op jit(solution)/shard_map/ppermute | solution.py:32
  87.3 22.0 %all_to_all.54 = f32[16,16,256]{2,0,1:T(8,128)S(1)} all-to-all(f32[16,16,256]{2,0,1:T(8,128)S(1)} %bitcast.82), channel_id=1, replica_groups=mesh['gx'=32,'gz'=16] {'gz'}, dimensions={1} | all-to-all | bytes 524288 | tf_op jit(solution)/shard_map/all_to_all | solution.py:165
  109.3 1.7 convolution_bitcast_fusion.1
  111.0 1.0 copy.31
  112.0 3.4 %all-to-all-start.1 = ((f32[256,1,256]{2,1,0:T(1,128)}), f32[256,1,256]{2,1,0:T(1,128)S(1)}, u32[]{:S(2)}, u32[]{:S(2)}) async-start(f32[256,1,256]{2,1,0:T(1,128)} %copy.31), calls=%async_computation.1 | async-start | bytes 524288 | tf_op jit(solution)/shard_map/all_to_all | solution.py:161
  115.5 11.1 %all-to-all-done.1 = f32[256,1,256]{2,1,0:T(1,128)S(1)} async-done(((f32[256,1,256]{2,1,0:T(1,128)}), f32[256,1,256]{2,1,0:T(1,128)S(1)}, u32[]{:S(2)}, u32[]{:S(2)}) %all-to-all-start.1) | async-done | bytes 262176 | tf_op jit(solution)/shard_map/all_to_all | solution.py:161
  127.0 1.3 collective-permute-start.16
  128.3 4.0 %collective-permute-start.17 = (f32[16,4,1,256]{3,0,2,1:T(8,128)S(1)}, f32[16,4,1,256]{3,0,2,1:T(8,128)S(1)}, u32[]{:S(2)}, u32[]{:S(2)}) collective-permute-start(f32[16,4,1,256]{3,0,2,1:T(8,128)S(1)} %get-tuple-element.45), channel_id=1, source_target_pairs={{0,16},{16,32},{32,48},{48,64},{64,80},{80,96},{96,112},{112,128},... | collective-permute-start | bytes 196616 | tf_op jit(solution)/shard_map/ppermute | solution.py:30
  132.6 1.0 collective-permute-done.17
  134.0 1.3 collective-permute-start.18
  135.3 4.6 %collective-permute-start.19 = (f32[16,4,1,256]{3,0,2,1:T(8,128)S(1)}, f32[16,4,1,256]{3,0,2,1:T(8,128)S(1)}, u32[]{:S(2)}, u32[]{:S(2)}) collective-permute-start(f32[16,4,1,256]{3,0,2,1:T(8,128)S(1)} %get-tuple-element.43), channel_id=1, source_target_pairs={{0,16},{16,32},{32,48},{48,64},{64,80},{80,96},{96,112},{112,128},... | collective-permute-start | bytes 196616 | tf_op jit(solution)/shard_map/ppermute | solution.py:30
  140.0 1.3 collective-permute-done.19
  141.7 1.3 collective-permute-start.20
  143.0 4.3 %collective-permute-start.21 = (f32[16,4,1,256]{3,0,2,1:T(8,128)S(1)}, f32[16,4,1,256]{3,0,2,1:T(8,128)S(1)}, u32[]{:S(2)}, u32[]{:S(2)}) collective-permute-start(f32[16,4,1,256]{3,0,2,1:T(8,128)S(1)} %get-tuple-element.41), channel_id=1, source_target_pairs={{0,16},{16,32},{32,48},{48,64},{64,80},{80,96},{96,112},{112,128},... | collective-permute-start | bytes 196616 | tf_op jit(solution)/shard_map/ppermute | solution.py:30
  147.3 1.3 collective-permute-done.21
  148.8 0.9 fusion.47
  149.7 6.4 %all-to-all-start.2 = ((f32[16,16,256]{2,0,1:T(8,128)}), f32[16,16,256]{2,0,1:T(8,128)S(1)}, u32[]{:S(2)}, u32[]{:S(2)}) async-start(f32[16,16,256]{2,0,1:T(8,128)} %bitcast.8), calls=%async_computation.2 | async-start | bytes 524288 | tf_op jit(solution)/shard_map/all_to_all | solution.py:165
  156.4 11.4 %all-to-all-done.2 = f32[16,16,256]{2,0,1:T(8,128)S(1)} async-done(((f32[16,16,256]{2,0,1:T(8,128)}), f32[16,16,256]{2,0,1:T(8,128)S(1)}, u32[]{:S(2)}, u32[]{:S(2)}) %all-to-all-start.2) | async-done | bytes 262176 | tf_op jit(solution)/shard_map/all_to_all | solution.py:165
  167.9 1.7 convolution_bitcast_fusion
  169.6 1.0 copy.32
  170.5 3.6 %all-to-all-start.3 = ((f32[256,1,256]{2,1,0:T(1,128)}), f32[256,1,256]{2,1,0:T(1,128)S(1)}, u32[]{:S(2)}, u32[]{:S(2)}) async-start(f32[256,1,256]{2,1,0:T(1,128)} %copy.32), calls=%async_computation.3 | async-start | bytes 524288 | tf_op jit(solution)/shard_map/all_to_all | solution.py:161
  174.2 10.8 %all-to-all-done.3 = f32[256,1,256]{2,1,0:T(1,128)S(1)} async-done(((f32[256,1,256]{2,1,0:T(1,128)}), f32[256,1,256]{2,1,0:T(1,128)S(1)}, u32[]{:S(2)}, u32[]{:S(2)}) %all-to-all-start.3) | async-done | bytes 262176 | tf_op jit(solution)/shard_map/all_to_all | solution.py:161
  185.1 4.0 %collective-permute-start.22 = (f32[1,16,4,1,256]{4,1,3,2,0:T(8,128)S(1)}, f32[1,16,4,1,256]{4,1,3,2,0:T(8,128)S(1)}, u32[]{:S(2)}, u32[]{:S(2)}) collective-permute-start(f32[1,16,4,1,256]{4,1,3,2,0:T(8,128)S(1)} %get-tuple-element.39), channel_id=1, source_target_pairs={{0,16},{16,32},{32,48},{48,64},{64,80},{80,96},{96,112},{112,128},... | collective-permute-start | bytes 196616 | tf_op jit(solution)/shard_map/ppermute | solution.py:30
  189.1 6.7 %collective-permute-start.23 = (f32[1,16,4,1,256]{4,1,3,2,0:T(8,128)S(1)}, f32[1,16,4,1,256]{4,1,3,2,0:T(8,128)S(1)}, u32[]{:S(2)}, u32[]{:S(2)}) collective-permute-start(f32[1,16,4,1,256]{4,1,3,2,0:T(8,128)S(1)} %get-tuple-element.40), channel_id=1, source_target_pairs={{16,0},{32,16},{48,32},{64,48},{80,64},{96,80},{112,96},{128,112},... | collective-permute-start | bytes 196616 | tf_op jit(solution)/shard_map/ppermute | solution.py:32
  196.5 1.0 collective-permute-done.23
  198.9 2.3 collective-permute-done.25
  202.5 3.7 %convolution_bitcast_fusion.3 = f32[4,4]{1,0:T(4,128)S(1)} fusion(f32[3,16,4,4,256]{4,1,3,2,0:T(8,128)S(1)} %get-tuple-element.16), kind=kOutput, calls=%fused_computation.19 | convolution fusion | flops 9437184 | bytes 786496 | tf_op jit(solution)/shard_map/czixy,czjxy->ij/dot_general | solution.py:207
  206.2 1.4 copy.41
  207.6 4.4 %fusion.3 = f32[4,4]{1,0:T(4,128)S(1)} fusion(f32[3,16,4,4,256]{4,1,3,2,0:T(8,128)S(1)} %get-tuple-element.17, pred[4,256]{1,0:T(4,128)(4,1)S(1)} %iota_compare_fusion.3, pred[4,16,4]{0,1,2:T(8,128)(4,1)S(1)} %broadcast_and_fusion, f32[4,3]{0,1:T(4,128)S(1)} %fusion.75), kind=kOutput, calls=%fused_computation.18 | convolution fusion | flops 9502800 | bytes 787824 | tf_op jit(solution)/shard_map/szxy,czjxy->scj/dot_general | solution.py:203
  212.6 36.6 %sum_all.1 = f32[8,128]{1,0:T(8,128)} custom-call(f32[8,128]{1,0:T(8,128)} %select_maximum_fusion.6.tile_ref), custom_call_target="tpu_custom_call" | custom-call | tf_op jit(solution)/shard_map/sum_all/pallas_call | solution.py:107
  249.2 1.3 slice_multiply_fusion
  250.5 2.6 %fusion.1 = f32[3,16,4,4,256]{4,2,3,1,0:T(4,128)S(1)} fusion(f32[3,16,4,4,256]{4,3,2,1,0:T(4,128)S(1)} %copy-done.1, f32[3,16,4,4,256]{4,1,3,2,0:T(8,128)S(1)} %get-tuple-element.17, f32[]{:T(128)S(6)} %mul.193, f32[8,128]{1,0:T(8,128)} %sum_all.1), kind=kOutput, calls=%fused_computation.13 | convolution fusion | flops 9830400 | bytes 2361348 | tf_op jit(solution)/shard_map/czjxy,ij->czixy/dot_general | solution.py:213
  253.1 1.1 copy.42
  (65 shorter events, 9.9 us)
Async XLA Ops:
  0.6 15.2 %copy-start.2 = (f32[16,4,256]{2,1,0:T(4,128)S(1)}, f32[16,4,256]{2,1,0:T(4,128)}, u32[]{:S(2)}) copy-start(f32[16,4,256]{2,1,0:T(4,128)} %param.8) | copy-start | bytes 196612
  5.8 11.2 %collective-permute-start = (f32[3,16,4,1,256]{4,1,3,2,0:T(8,128)S(1)}, f32[3,16,4,1,256]{4,1,3,2,0:T(8,128)S(1)}, u32[]{:S(2)}, u32[]{:S(2)}) collective-permute-start(f32[3,16,4,1,256]{4,1,3,2,0:T(8,128)S(1)} %get-tuple-element.35), channel_id=1, source_target_pairs={{0,16},{16,32},{32,48},{48,64},{64,80},{80,96},{96,112},{112,128},... | collective-permute-start | bytes 589832 | tf_op jit(solution)/shard_map/ppermute | solution.py:30
  9.7 8.7 %collective-permute-start.1 = (f32[3,16,4,1,256]{4,1,3,2,0:T(8,128)S(1)}, f32[3,16,4,1,256]{4,1,3,2,0:T(8,128)S(1)}, u32[]{:S(2)}, u32[]{:S(2)}) collective-permute-start(f32[3,16,4,1,256]{4,1,3,2,0:T(8,128)S(1)} %get-tuple-element.36), channel_id=1, source_target_pairs={{16,0},{32,16},{48,32},{64,48},{80,64},{96,80},{112,96},{128,112},... | collective-permute-start | bytes 589832 | tf_op jit(solution)/shard_map/ppermute | solution.py:32
  18.5 8.7 %copy-start = (f32[3,16,4,4,256]{4,3,2,1,0:T(4,128)S(1)}, f32[3,16,4,4,256]{4,3,2,1,0:T(4,128)}, u32[]{:S(2)}) copy-start(f32[3,16,4,4,256]{4,3,2,1,0:T(4,128)} %param.6) | copy-start | bytes 2359300
  18.5 7.3 %collective-permute-start.2 = (f32[3,1,4,6,256]{4,1,3,2,0:T(1,128)S(1)}, f32[3,1,4,6,256]{4,1,3,2,0:T(1,128)S(1)}, u32[]{:S(2)}, u32[]{:S(2)}) collective-permute-start(f32[3,1,4,6,256]{4,1,3,2,0:T(1,128)S(1)} %get-tuple-element.24), channel_id=1, source_target_pairs={{0,1},{1,2},{2,3},{3,4},{4,5},{5,6},{6,7},{7,8},{8,9},{9,10},{10,1... | collective-permute-start | bytes 221192 | tf_op jit(solution)/shard_map/ppermute | solution.py:30
  23.0 3.8 %collective-permute-start.3 = (f32[3,1,4,6,256]{4,1,3,2,0:T(1,128)S(1)}, f32[3,1,4,6,256]{4,1,3,2,0:T(1,128)S(1)}, u32[]{:S(2)}, u32[]{:S(2)}) collective-permute-start(f32[3,1,4,6,256]{4,1,3,2,0:T(1,128)S(1)} %get-tuple-element.25), channel_id=1, source_target_pairs={{1,0},{2,1},{3,2},{4,3},{5,4},{6,5},{7,6},{8,7},{9,8},{10,9},{11,1... | collective-permute-start | bytes 221192 | tf_op jit(solution)/shard_map/ppermute | solution.py:32
  28.4 10.5 %collective-permute-start.4 = (f32[3,16,4,1,256]{4,1,3,2,0:T(8,128)S(1)}, f32[3,16,4,1,256]{4,1,3,2,0:T(8,128)S(1)}, u32[]{:S(2)}, u32[]{:S(2)}) collective-permute-start(f32[3,16,4,1,256]{4,1,3,2,0:T(8,128)S(1)} %get-tuple-element.33), channel_id=1, source_target_pairs={{0,16},{16,32},{32,48},{48,64},{64,80},{80,96},{96,112},{112,128},... | collective-permute-start | bytes 589832 | tf_op jit(solution)/shard_map/ppermute | solution.py:30
  30.4 10.0 %collective-permute-start.5 = (f32[3,16,4,1,256]{4,1,3,2,0:T(8,128)S(1)}, f32[3,16,4,1,256]{4,1,3,2,0:T(8,128)S(1)}, u32[]{:S(2)}, u32[]{:S(2)}) collective-permute-start(f32[3,16,4,1,256]{4,1,3,2,0:T(8,128)S(1)} %get-tuple-element.34), channel_id=1, source_target_pairs={{16,0},{32,16},{48,32},{64,48},{80,64},{96,80},{112,96},{128,112},... | collective-permute-start | bytes 589832 | tf_op jit(solution)/shard_map/ppermute | solution.py:32
  40.5 5.5 %collective-permute-start.6 = (f32[3,1,4,6,256]{4,1,3,2,0:T(1,128)S(1)}, f32[3,1,4,6,256]{4,1,3,2,0:T(1,128)S(1)}, u32[]{:S(2)}, u32[]{:S(2)}) collective-permute-start(f32[3,1,4,6,256]{4,1,3,2,0:T(1,128)S(1)} %get-tuple-element.22), channel_id=1, source_target_pairs={{0,1},{1,2},{2,3},{3,4},{4,5},{5,6},{6,7},{7,8},{8,9},{9,10},{10,1... | collective-permute-start | bytes 221192 | tf_op jit(solution)/shard_map/ppermute | solution.py:30
  42.0 4.3 %collective-permute-start.7 = (f32[3,1,4,6,256]{4,1,3,2,0:T(1,128)S(1)}, f32[3,1,4,6,256]{4,1,3,2,0:T(1,128)S(1)}, u32[]{:S(2)}, u32[]{:S(2)}) collective-permute-start(f32[3,1,4,6,256]{4,1,3,2,0:T(1,128)S(1)} %get-tuple-element.23), channel_id=1, source_target_pairs={{1,0},{2,1},{3,2},{4,3},{5,4},{6,5},{7,6},{8,7},{9,8},{10,9},{11,1... | collective-permute-start | bytes 221192 | tf_op jit(solution)/shard_map/ppermute | solution.py:32
  47.8 10.5 %collective-permute-start.8 = (f32[3,16,4,1,256]{4,1,3,2,0:T(8,128)S(1)}, f32[3,16,4,1,256]{4,1,3,2,0:T(8,128)S(1)}, u32[]{:S(2)}, u32[]{:S(2)}) collective-permute-start(f32[3,16,4,1,256]{4,1,3,2,0:T(8,128)S(1)} %get-tuple-element.31), channel_id=1, source_target_pairs={{0,16},{16,32},{32,48},{48,64},{64,80},{80,96},{96,112},{112,128},... | collective-permute-start | bytes 589832 | tf_op jit(solution)/shard_map/ppermute | solution.py:30
  49.8 10.0 %collective-permute-start.9 = (f32[3,16,4,1,256]{4,1,3,2,0:T(8,128)S(1)}, f32[3,16,4,1,256]{4,1,3,2,0:T(8,128)S(1)}, u32[]{:S(2)}, u32[]{:S(2)}) collective-permute-start(f32[3,16,4,1,256]{4,1,3,2,0:T(8,128)S(1)} %get-tuple-element.32), channel_id=1, source_target_pairs={{16,0},{32,16},{48,32},{64,48},{80,64},{96,80},{112,96},{128,112},... | collective-permute-start | bytes 589832 | tf_op jit(solution)/shard_map/ppermute | solution.py:32
  59.9 6.2 %collective-permute-start.10 = (f32[3,1,4,6,256]{4,1,3,2,0:T(1,128)S(1)}, f32[3,1,4,6,256]{4,1,3,2,0:T(1,128)S(1)}, u32[]{:S(2)}, u32[]{:S(2)}) collective-permute-start(f32[3,1,4,6,256]{4,1,3,2,0:T(1,128)S(1)} %get-tuple-element.20), channel_id=1, source_target_pairs={{0,1},{1,2},{2,3},{3,4},{4,5},{5,6},{6,7},{7,8},{8,9},{9,10},{10,1... | collective-permute-start | bytes 221192 | tf_op jit(solution)/shard_map/ppermute | solution.py:30
  60.9 5.4 %collective-permute-start.11 = (f32[3,1,4,6,256]{4,1,3,2,0:T(1,128)S(1)}, f32[3,1,4,6,256]{4,1,3,2,0:T(1,128)S(1)}, u32[]{:S(2)}, u32[]{:S(2)}) collective-permute-start(f32[3,1,4,6,256]{4,1,3,2,0:T(1,128)S(1)} %get-tuple-element.21), channel_id=1, source_target_pairs={{1,0},{2,1},{3,2},{4,3},{5,4},{6,5},{7,6},{8,7},{9,8},{10,9},{11,1... | collective-permute-start | bytes 221192 | tf_op jit(solution)/shard_map/ppermute | solution.py:32
  67.9 10.5 %collective-permute-start.12 = (f32[3,16,4,1,256]{4,1,3,2,0:T(8,128)S(1)}, f32[3,16,4,1,256]{4,1,3,2,0:T(8,128)S(1)}, u32[]{:S(2)}, u32[]{:S(2)}) collective-permute-start(f32[3,16,4,1,256]{4,1,3,2,0:T(8,128)S(1)} %get-tuple-element.29), channel_id=1, source_target_pairs={{0,16},{16,32},{32,48},{48,64},{64,80},{80,96},{96,112},{112,128},... | collective-permute-start | bytes 589832 | tf_op jit(solution)/shard_map/ppermute | solution.py:30
  69.8 10.0 %collective-permute-start.13 = (f32[3,16,4,1,256]{4,1,3,2,0:T(8,128)S(1)}, f32[3,16,4,1,256]{4,1,3,2,0:T(8,128)S(1)}, u32[]{:S(2)}, u32[]{:S(2)}) collective-permute-start(f32[3,16,4,1,256]{4,1,3,2,0:T(8,128)S(1)} %get-tuple-element.30), channel_id=1, source_target_pairs={{16,0},{32,16},{48,32},{64,48},{80,64},{96,80},{112,96},{128,112},... | collective-permute-start | bytes 589832 | tf_op jit(solution)/shard_map/ppermute | solution.py:32
  79.9 6.6 %collective-permute-start.14 = (f32[3,1,4,6,256]{4,1,3,2,0:T(1,128)S(1)}, f32[3,1,4,6,256]{4,1,3,2,0:T(1,128)S(1)}, u32[]{:S(2)}, u32[]{:S(2)}) collective-permute-start(f32[3,1,4,6,256]{4,1,3,2,0:T(1,128)S(1)} %get-tuple-element.18), channel_id=1, source_target_pairs={{0,1},{1,2},{2,3},{3,4},{4,5},{5,6},{6,7},{7,8},{8,9},{9,10},{10,1... | collective-permute-start | bytes 221192 | tf_op jit(solution)/shard_map/ppermute | solution.py:30
  80.0 6.7 %collective-permute-start.15 = (f32[3,1,4,6,256]{4,1,3,2,0:T(1,128)S(1)}, f32[3,1,4,6,256]{4,1,3,2,0:T(1,128)S(1)}, u32[]{:S(2)}, u32[]{:S(2)}) collective-permute-start(f32[3,1,4,6,256]{4,1,3,2,0:T(1,128)S(1)} %get-tuple-element.19), channel_id=1, source_target_pairs={{1,0},{2,1},{3,2},{4,3},{5,4},{6,5},{7,6},{8,7},{9,8},{10,9},{11,1... | collective-permute-start | bytes 221192 | tf_op jit(solution)/shard_map/ppermute | solution.py:32
  112.0 14.6 %all-to-all-start.1 = ((f32[256,1,256]{2,1,0:T(1,128)}), f32[256,1,256]{2,1,0:T(1,128)S(1)}, u32[]{:S(2)}, u32[]{:S(2)}) async-start(f32[256,1,256]{2,1,0:T(1,128)} %copy.31), calls=%async_computation.1 | async-start | bytes 524288 | tf_op jit(solution)/shard_map/all_to_all | solution.py:161
  127.0 5.6 %collective-permute-start.16 = (f32[16,4,1,256]{3,0,2,1:T(8,128)S(1)}, f32[16,4,1,256]{3,0,2,1:T(8,128)S(1)}, u32[]{:S(2)}, u32[]{:S(2)}) collective-permute-start(f32[16,4,1,256]{3,0,2,1:T(8,128)S(1)} %get-tuple-element.46), channel_id=1, source_target_pairs={{16,0},{32,16},{48,32},{64,48},{80,64},{96,80},{112,96},{128,112},... | collective-permute-start | bytes 196616 | tf_op jit(solution)/shard_map/ppermute | solution.py:32
  128.3 5.3 %collective-permute-start.17 = (f32[16,4,1,256]{3,0,2,1:T(8,128)S(1)}, f32[16,4,1,256]{3,0,2,1:T(8,128)S(1)}, u32[]{:S(2)}, u32[]{:S(2)}) collective-permute-start(f32[16,4,1,256]{3,0,2,1:T(8,128)S(1)} %get-tuple-element.45), channel_id=1, source_target_pairs={{0,16},{16,32},{32,48},{48,64},{64,80},{80,96},{96,112},{112,128},... | collective-permute-start | bytes 196616 | tf_op jit(solution)/shard_map/ppermute | solution.py:30
  134.0 6.0 %collective-permute-start.18 = (f32[16,4,1,256]{3,0,2,1:T(8,128)S(1)}, f32[16,4,1,256]{3,0,2,1:T(8,128)S(1)}, u32[]{:S(2)}, u32[]{:S(2)}) collective-permute-start(f32[16,4,1,256]{3,0,2,1:T(8,128)S(1)} %get-tuple-element.44), channel_id=1, source_target_pairs={{16,0},{32,16},{48,32},{64,48},{80,64},{96,80},{112,96},{128,112},... | collective-permute-start | bytes 196616 | tf_op jit(solution)/shard_map/ppermute | solution.py:32
  135.3 6.0 %collective-permute-start.19 = (f32[16,4,1,256]{3,0,2,1:T(8,128)S(1)}, f32[16,4,1,256]{3,0,2,1:T(8,128)S(1)}, u32[]{:S(2)}, u32[]{:S(2)}) collective-permute-start(f32[16,4,1,256]{3,0,2,1:T(8,128)S(1)} %get-tuple-element.43), channel_id=1, source_target_pairs={{0,16},{16,32},{32,48},{48,64},{64,80},{80,96},{96,112},{112,128},... | collective-permute-start | bytes 196616 | tf_op jit(solution)/shard_map/ppermute | solution.py:30
  141.7 14.5 %copy-start.3 = (s32[4,4]{1,0:T(4,128)S(1)}, s32[4,4]{1,0:T(4,128)}, u32[]{:S(2)}) copy-start(s32[4,4]{1,0:T(4,128)} %param.10) | copy-start | bytes 196
  141.7 5.6 %collective-permute-start.20 = (f32[16,4,1,256]{3,0,2,1:T(8,128)S(1)}, f32[16,4,1,256]{3,0,2,1:T(8,128)S(1)}, u32[]{:S(2)}, u32[]{:S(2)}) collective-permute-start(f32[16,4,1,256]{3,0,2,1:T(8,128)S(1)} %get-tuple-element.42), channel_id=1, source_target_pairs={{16,0},{32,16},{48,32},{64,48},{80,64},{96,80},{112,96},{128,112},... | collective-permute-start | bytes 196616 | tf_op jit(solution)/shard_map/ppermute | solution.py:32
  143.0 5.6 %collective-permute-start.21 = (f32[16,4,1,256]{3,0,2,1:T(8,128)S(1)}, f32[16,4,1,256]{3,0,2,1:T(8,128)S(1)}, u32[]{:S(2)}, u32[]{:S(2)}) collective-permute-start(f32[16,4,1,256]{3,0,2,1:T(8,128)S(1)} %get-tuple-element.41), channel_id=1, source_target_pairs={{0,16},{16,32},{32,48},{48,64},{64,80},{80,96},{96,112},{112,128},... | collective-permute-start | bytes 196616 | tf_op jit(solution)/shard_map/ppermute | solution.py:30
  149.7 18.1 %all-to-all-start.2 = ((f32[16,16,256]{2,0,1:T(8,128)}), f32[16,16,256]{2,0,1:T(8,128)S(1)}, u32[]{:S(2)}, u32[]{:S(2)}) async-start(f32[16,16,256]{2,0,1:T(8,128)} %bitcast.8), calls=%async_computation.2 | async-start | bytes 524288 | tf_op jit(solution)/shard_map/all_to_all | solution.py:165
  170.5 14.5 %all-to-all-start.3 = ((f32[256,1,256]{2,1,0:T(1,128)}), f32[256,1,256]{2,1,0:T(1,128)S(1)}, u32[]{:S(2)}, u32[]{:S(2)}) async-start(f32[256,1,256]{2,1,0:T(1,128)} %copy.32), calls=%async_computation.3 | async-start | bytes 524288 | tf_op jit(solution)/shard_map/all_to_all | solution.py:161
  185.1 11.3 %collective-permute-start.22 = (f32[1,16,4,1,256]{4,1,3,2,0:T(8,128)S(1)}, f32[1,16,4,1,256]{4,1,3,2,0:T(8,128)S(1)}, u32[]{:S(2)}, u32[]{:S(2)}) collective-permute-start(f32[1,16,4,1,256]{4,1,3,2,0:T(8,128)S(1)} %get-tuple-element.39), channel_id=1, source_target_pairs={{0,16},{16,32},{32,48},{48,64},{64,80},{80,96},{96,112},{112,128},... | collective-permute-start | bytes 196616 | tf_op jit(solution)/shard_map/ppermute | solution.py:30
  189.1 8.3 %collective-permute-start.23 = (f32[1,16,4,1,256]{4,1,3,2,0:T(8,128)S(1)}, f32[1,16,4,1,256]{4,1,3,2,0:T(8,128)S(1)}, u32[]{:S(2)}, u32[]{:S(2)}) collective-permute-start(f32[1,16,4,1,256]{4,1,3,2,0:T(8,128)S(1)} %get-tuple-element.40), channel_id=1, source_target_pairs={{16,0},{32,16},{48,32},{64,48},{80,64},{96,80},{112,96},{128,112},... | collective-permute-start | bytes 196616 | tf_op jit(solution)/shard_map/ppermute | solution.py:32
  197.5 1.4 collective-permute-start.24
  197.9 3.3 %collective-permute-start.25 = (f32[1,1,4,6,256]{4,1,3,2,0:T(1,128)S(1)}, f32[1,1,4,6,256]{4,1,3,2,0:T(1,128)S(1)}, u32[]{:S(2)}, u32[]{:S(2)}) collective-permute-start(f32[1,1,4,6,256]{4,1,3,2,0:T(1,128)S(1)} %get-tuple-element.38), channel_id=1, source_target_pairs={{1,0},{2,1},{3,2},{4,3},{5,4},{6,5},{7,6},{8,7},{9,8},{10,9},{11,1... | collective-permute-start | bytes 73736 | tf_op jit(solution)/shard_map/ppermute | solution.py:32
  202.4 48.0 %copy-start.1 = (f32[3,16,4,4,256]{4,3,2,1,0:T(4,128)S(1)}, f32[3,16,4,4,256]{4,3,2,1,0:T(4,128)}, u32[]{:S(2)}) copy-start(f32[3,16,4,4,256]{4,3,2,1,0:T(4,128)} %param.7) | copy-start | bytes 2359300

commit v2 on v0

v2 whole, which is shorter than its diff:
```python
import functools
import math

import jax
import jax.numpy as jnp
import numpy as np
from jax import lax
from jax.experimental import pallas as pl
from jax.experimental.pallas import tpu as pltpu
from jax.sharding import PartitionSpec as P

SWEEPS = 3
POISSON = 4
SHIFTS = 8


viscosity = 0.4
shift_table = (0.6, 0.8, 1.0, 1.25, 1.6, 2.0, 2.5, 3.2)
chebyshev_weights = (1.0 / 1.9352976, 1.0 / 1.4752809, 1.0 / 0.8247191, 1.0 / 0.3647024)
highest = lax.Precision.HIGHEST


def step_kernel(
    sizes,
    shift_ref,
    cells_ref,
    factor_ref,
    base_ref,
    table_ref,
    scale_ref,
    solved_ref,
    out_ref,
    fields,
    inverse,
    row_sends,
    row_halos,
    blocks,
    planes,
    rhs,
    modes,
    beside,
    pressure,
    pressure_row,
    pressure_halo,
    slots_z,
    slots_x,
    slots_y,
    mid,
    halo_send,
    halo_recv,
    turn_send,
    turn_recv,
    mode_send,
    mode_recv,
    sum_send,
    sum_recv,
):
    count_z, count_x, count_y = sizes
    count_gx = count_x * count_y
    components, stream_cells, columns, span_cells, normal_cells = factor_ref.shape
    last_cell = stream_cells - 1
    cells = stream_cells * columns
    gx, gz = lax.axis_index("gx"), lax.axis_index("gz")
    here_x, here_y = gx % count_x, gx // count_x
    next_gx = ((gx + 1) % count_gx, gz)
    before_gx = ((gx + count_gx - 1) % count_gx, gz)
    next_gz = (gx, (gz + 1) % count_z)
    before_gz = (gx, (gz + count_z - 1) % count_z)
    shift = shift_ref[0]

    odd = gx % 2
    turn = 1 - 2 * odd

    def mirrored(cell):
        return odd * last_cell + turn * cell

    plane_cell = mirrored(gz % stream_cells)
    plane_column = gz // stream_cells
    at_end = plane_cell // last_cell
    at_start = (last_cell - plane_cell) // last_cell
    plane_next = ((gx + at_end) % count_gx, gz + turn * (1 - at_end))
    plane_before = ((gx + count_gx - at_start) % count_gx, gz - turn * (1 - at_start))

    def low(cell):
        return jnp.where(gx + cell == 0, 0.0, 1.0)

    def high(cell):
        return jnp.where(count_gx - 1 - gx + last_cell - cell == 0, 0.0, 1.0)

    def partner(stage, offset):
        if stage == 0:
            return (gx, (gz + offset) % count_z)
        if stage == 1:
            return (here_y * count_x + (here_x + offset) % count_x, gz)
        return ((here_y + offset) % count_y * count_x + here_x, gz)

    def remote(src, dst, send, recv, device):
        return pltpu.make_async_remote_copy(
            src_ref=src,
            dst_ref=dst,
            send_sem=send,
            recv_sem=recv,
            device_id=device,
            device_id_type=pl.DeviceIdType.MESH,
        )

    def loop(first, end, act):
        def run(index, carry):
            act(index)
            return carry

        lax.fori_loop(first, end, run, 0)

    counts = (count_z, count_x, count_y)
    barrier = pltpu.get_barrier_semaphore()

    def greet(device):
        pl.semaphore_signal(barrier, inc=1, device_id=device, device_id_type=pl.DeviceIdType.MESH)

    for stage in range(3):
        loop(1, counts[stage], lambda offset, stage=stage: greet(partner(stage, offset)))
    greet(next_gx)
    greet(before_gx)

    rows = lax.broadcasted_iota(jnp.int32, (span_cells, normal_cells), 0)
    lanes = lax.broadcasted_iota(jnp.int32, (span_cells, normal_cells), 1)

    def normal_before(block):
        return jnp.where(lanes == 0, 0.0, pltpu.roll(block, 1, 1))

    def normal_after(block):
        return jnp.where(lanes == normal_cells - 1, 0.0, pltpu.roll(block, normal_cells - 1, 1))

    def span_before(block, halo):
        return jnp.where(rows == 0, halo, pltpu.roll(block, 1, 0))

    def span_after(block, halo):
        return jnp.where(rows == span_cells - 1, halo, pltpu.roll(block, span_cells - 1, 0))

    def halo_copies(level, part):
        moves = (
            (fields.at[level, part, stream_cells], fields.at[level, part, 0], next_gx),
            (fields.at[level, part, 1], fields.at[level, part, stream_cells + 1], before_gx),
            (row_sends.at[level, part, 0], row_halos.at[level, part, 0], next_gz),
            (row_sends.at[level, part, 1], row_halos.at[level, part, 1], before_gz),
        )
        sides = (0, 1, 2, 3) if level < SWEEPS else ((0,), (), (2,))[part]
        copies = []
        for side in sides:
            src, dst, device = moves[side]
            copies.append(
                remote(src, dst, halo_send.at[level, part, side], halo_recv.at[level, part, side], device)
            )
        return copies

    def keep(level, part, index, block):
        cell, column = lax.div(index, columns), lax.rem(index, columns)
        fields[level, part, cell + 1, column] = block
        row_sends[level, part, 0, index] = block[span_cells - 1 :]
        row_sends[level, part, 1, index] = block[:1]

    def invert(cell):
        inverse[cell] = 1.0 / (shift + 6.0 * viscosity + base_ref[cell])

    loop(0, stream_cells, invert)
    for part in range(components):
        def first_guess(index, part=part):
            cell, column = lax.div(index, columns), lax.rem(index, columns)
            keep(0, part, index, -factor_ref[part, cell, column] * inverse[cell])

        loop(0, cells, first_guess)
        if part == 0:
            pl.semaphore_wait(barrier, sum(counts) - 3 + 2)
        for copy in halo_copies(0, part):
            copy.start()
    for level in range(SWEEPS):
        for part in range(components):
            for copy in halo_copies(level, part):
                copy.wait()

            def sweep(index, level=level, part=part):
                cell, column = lax.div(index, columns), lax.rem(index, columns)
                block = fields[level, part, cell + 1, column]
                behind = fields[level, part, cell, column] * low(cell)
                around = behind + fields[level, part, cell + 2, column] * high(cell)
                around = around + normal_before(block) + normal_after(block)
                around = around + span_before(block, row_halos[level, part, 0, index])
                around = around + span_after(block, row_halos[level, part, 1, index])
                total = viscosity * around + base_ref[cell] * behind - factor_ref[part, cell, column]
                keep(level + 1, part, index, total * inverse[cell])

            loop(0, cells, sweep)
            for copy in halo_copies(level + 1, part):
                copy.start()
    for part in range(components):
        for copy in halo_copies(SWEEPS, part):
            copy.wait()

    def diverge(index):
        cell, column = lax.div(index, columns), lax.rem(index, columns)
        normal = fields[SWEEPS, 1, cell + 1, column]
        span = fields[SWEEPS, 2, cell + 1, column]
        total = 2.0 * (
            fields[SWEEPS, 0, cell + 1, column] - fields[SWEEPS, 0, cell, column] * low(cell)
        )
        total = total + (normal - normal_before(normal))
        total = total + (span - span_before(span, row_halos[SWEEPS, 2, 0, index]))
        blocks[column * stream_cells + mirrored(cell)] = -total

    loop(0, cells, diverge)

    def gather_copy(offset):
        device = partner(0, offset)
        return remote(
            blocks.at[device[1]], planes.at[gz], turn_send.at[0, offset], turn_recv.at[0, offset], device
        )

    loop(1, count_z, lambda offset: gather_copy(offset).start())
    planes[gz] = blocks[gz]
    loop(1, count_z, lambda offset: gather_copy(offset).wait())
    span_total = count_z * span_cells
    whole = planes[...].reshape(span_total, normal_cells)
    spectrum = jnp.dot(
        table_ref[...], whole, precision=highest, preferred_element_type=jnp.float32
    ) * scale_ref[...]
    shape = (count_z, span_cells, normal_cells)
    rhs[...] = spectrum.reshape(shape)
    modes[0] = (chebyshev_weights[0] * spectrum).reshape(shape)

    def mode_copies(level):
        return (
            remote(
                modes.at[level], beside.at[level, 0], mode_send.at[level, 0], mode_recv.at[level, 0], plane_next
            ),
            remote(
                modes.at[level], beside.at[level, 1], mode_send.at[level, 1], mode_recv.at[level, 1], plane_before
            ),
        )

    plane_low, plane_high = 4.0 * low(plane_cell), 4.0 * high(plane_cell)
    for level in range(POISSON - 1):
        for copy in mode_copies(level):
            copy.start()
        for copy in mode_copies(level):
            copy.wait()
        weight = chebyshev_weights[level + 1]

        def smooth(index, level=level, weight=weight):
            block = modes[level, index]
            around = plane_low * beside[level, 0, index] + plane_high * beside[level, 1, index]
            around = around + normal_before(block) + normal_after(block)
            scale = scale_ref[pl.ds(pl.multiple_of(index * span_cells, span_cells), span_cells), :]
            modes[level + 1, index] = (1.0 - weight) * block + weight * (rhs[index] + scale * around)

        loop(0, count_z, smooth)
    whole = modes[POISSON - 1].reshape(span_total, normal_cells)
    back = jnp.dot(table_ref[...], whole, precision=highest, preferred_element_type=jnp.float32)
    rhs[...] = back.reshape(shape)

    def scatter_copy(offset):
        device = partner(0, offset)
        return remote(
            rhs.at[device[1]],
            pressure.at[plane_cell, plane_column],
            turn_send.at[1, offset],
            turn_recv.at[1, offset],
            device,
        )

    loop(1, count_z, lambda offset: scatter_copy(offset).start())
    pressure[plane_cell, plane_column] = rhs[gz]
    loop(1, count_z, lambda offset: scatter_copy(offset).wait())

    def first_row(index):
        cell, column = lax.div(index, columns), lax.rem(index, columns)
        pressure_row[index] = pressure[cell, column][:1]

    loop(0, cells, first_row)
    copies = (
        remote(pressure.at[0], pressure.at[stream_cells], mode_send.at[POISSON - 1, 0], mode_recv.at[POISSON - 1, 0], before_gx),
        remote(pressure_row, pressure_halo, mode_send.at[POISSON - 1, 1], mode_recv.at[POISSON - 1, 1], before_gz),
    )
    for copy in copies:
        copy.start()
    for copy in copies:
        copy.wait()

    pairs = [(i, j) for i in range(columns) for j in range(i, columns)]
    half = normal_cells // 2

    def finish(cell, sums):
        updated = []
        for column in range(columns):
            block = pressure[cell, column]
            gradient = (
                2.0 * (pressure[cell + 1, column] * high(cell) - block),
                normal_after(block) - block,
                span_after(block, pressure_halo[cell * columns + column]) - block,
            )
            updated.append([])
            for part in range(components):
                value = fields[SWEEPS, part, cell + 1, column] - gradient[part]
                solved_ref[part, cell, column] = value
                updated[column].append(factor_ref[part, cell, column] + 2.0 * shift * value)
        totals = []
        for total, (i, j) in zip(sums, pairs):
            product = updated[i][0] * updated[j][0]
            for part in range(1, components):
                product = product + updated[i][part] * updated[j][part]
            product = product[:, :half] + product[:, half:]
            totals.append(total + product[:8] + product[8:])
        return tuple(totals)

    zero = jnp.zeros((8, half), jnp.float32)
    sums = lax.fori_loop(0, stream_cells, finish, (zero,) * len(pairs))
    tile_rows = lax.broadcasted_iota(jnp.int32, (8, 128), 0)
    tile_lanes = lax.broadcasted_iota(jnp.int32, (8, 128), 1)
    tile = jnp.zeros((8, 128), jnp.float32)

    def put(tile, row, lane, value):
        return jnp.where((tile_rows == row) & (tile_lanes == lane), value, tile)

    for total, (i, j) in zip(sums, pairs):
        value = jnp.sum(jnp.sum(total, axis=1, keepdims=True), axis=0, keepdims=True)
        tile = put(tile, i, j, value)
        if i != j:
            tile = put(tile, j, i, value)
    line_lanes = lax.broadcasted_iota(jnp.int32, (1, normal_cells), 1)
    for sensor in range(cells_ref.shape[0]):
        part = jnp.clip(cells_ref[sensor, 0], 0, components - 1)
        span = cells_ref[sensor, 1] - gz * span_cells
        stream = cells_ref[sensor, 2] - gx * stream_cells
        inside = (span >= 0) & (span < span_cells) & (stream >= 0) & (stream < stream_cells)
        span = jnp.clip(span, 0, span_cells - 1)
        stream = jnp.clip(stream, 0, stream_cells - 1)
        chosen = (line_lanes == cells_ref[sensor, 3]) & inside
        for column in range(columns):
            line = solved_ref[part, stream, column, pl.ds(span, 1), :]
            value = jnp.sum(jnp.where(chosen, line, 0.0), axis=1, keepdims=True)
            tile = put(tile, columns + sensor, column, value)
    mid[0] = tile
    places = (gz, here_x, here_y)
    bases = (0, count_z, count_z + count_x)
    for stage, slots in enumerate((slots_z, slots_x, slots_y)):
        def sum_copy(offset, stage=stage, slots=slots):
            index = bases[stage] + offset
            return remote(
                mid.at[stage], slots.at[places[stage]], sum_send.at[index], sum_recv.at[index], partner(stage, offset)
            )

        loop(1, counts[stage], lambda offset, sum_copy=sum_copy: sum_copy(offset).start())
        slots[places[stage]] = mid[stage]
        loop(1, counts[stage], lambda offset, sum_copy=sum_copy: sum_copy(offset).wait())
        total = slots[0]
        for place in range(1, counts[stage]):
            total = total + slots[place]
        if stage < 2:
            mid[stage + 1] = total
        else:
            out_ref[...] = total


def hartley_table(span_total):
    index = np.arange(span_total)
    angles = 2.0 * math.pi * (index[:, None] * index[None, :] % span_total) / span_total
    return ((np.cos(angles) + np.sin(angles)) / math.sqrt(span_total)).astype(np.float32)


def mode_scale(span_total, normal_cells):
    wavenumber = 2.0 * math.pi * np.arange(span_total) / span_total
    diagonal = 10.0 + (2.0 - 2.0 * np.cos(wavenumber))
    return np.repeat((1.0 / diagonal).astype(np.float32)[:, None], normal_cells, axis=1)


def solve(shift, sensor_cells, turned_factor, turned_base, sizes):
    count_z, count_x, count_y = sizes
    components, stream_cells, columns, span_cells, normal_cells = turned_factor.shape
    cells = stream_cells * columns
    span_total = count_z * span_cells
    vmem = pl.BlockSpec(memory_space=pltpu.VMEM)
    smem = pl.BlockSpec(memory_space=pltpu.SMEM)
    f32 = jnp.float32
    group = (count_z, span_cells, normal_cells)
    dma = pltpu.SemaphoreType.DMA
    return pl.pallas_call(
        functools.partial(step_kernel, sizes),
        out_shape=(
            jax.ShapeDtypeStruct(turned_factor.shape, f32),
            jax.ShapeDtypeStruct((8, 128), f32),
        ),
        in_specs=[smem, smem, vmem, vmem, vmem, vmem],
        out_specs=(vmem, vmem),
        scratch_shapes=[
            pltpu.VMEM((SWEEPS + 1, components, stream_cells + 2, columns, span_cells, normal_cells), f32),
            pltpu.VMEM((stream_cells, span_cells, normal_cells), f32),
            pltpu.VMEM((SWEEPS + 1, components, 2, cells, 1, normal_cells), f32),
            pltpu.VMEM((SWEEPS + 1, components, 2, cells, 1, normal_cells), f32),
            pltpu.VMEM(group, f32),
            pltpu.VMEM(group, f32),
            pltpu.VMEM(group, f32),
            pltpu.VMEM((POISSON,) + group, f32),
            pltpu.VMEM((POISSON - 1, 2) + group, f32),
            pltpu.VMEM((stream_cells + 1, columns, span_cells, normal_cells), f32),
            pltpu.VMEM((cells, 1, normal_cells), f32),
            pltpu.VMEM((cells, 1, normal_cells), f32),
        ]
        + [pltpu.VMEM((size, 8, 128), f32) for size in sizes]
        + [
            pltpu.VMEM((3, 8, 128), f32),
            dma((SWEEPS + 1, components, 4)),
            dma((SWEEPS + 1, components, 4)),
            dma((2, count_z)),
            dma((2, count_z)),
            dma((POISSON, 2)),
            dma((POISSON, 2)),
            dma((sum(sizes),)),
            dma((sum(sizes),)),
        ],
        compiler_params=pltpu.CompilerParams(collective_id=0, has_side_effects=True),
        name="solve",
    )(
        shift,
        sensor_cells,
        turned_factor,
        turned_base,
        jnp.asarray(hartley_table(span_total)),
        jnp.asarray(mode_scale(span_total, normal_cells)),
    )


def shards(factor, gain, base_flow, shift_index, sensor_cells):
    components, span_cells, columns, stream_cells, normal_cells = factor.shape
    count_gx, count_z = lax.axis_size("gx"), lax.axis_size("gz")
    count_x = 4 if count_gx % 4 == 0 else count_gx
    sizes = (count_z, count_x, count_gx // count_x)
    shift_values = jnp.asarray(shift_table, jnp.float32)
    shift_value = jnp.sum(jnp.where(jnp.arange(SHIFTS) == shift_index[0], shift_values, 0.0))
    solved, tile = solve(
        shift_value[None],
        sensor_cells,
        jnp.transpose(factor, (0, 3, 2, 1, 4)),
        jnp.transpose(base_flow, (1, 0, 2)),
        sizes,
    )
    solved = jnp.transpose(solved, (0, 3, 2, 1, 4))
    gram_total, readout = tile[:columns, :columns], tile[columns : 2 * columns, :columns]
    new_factor = factor + 2.0 * shift_value * solved
    total_cells = components * stream_cells * count_gx * normal_cells * span_cells * count_z
    gram = gram_total / float(total_cells)
    added = solved[:, :, 0:1] * readout[None, None, :, 0, None, None]
    for column in range(1, columns):
        added = added + solved[:, :, column : column + 1] * readout[None, None, :, column, None, None]
    new_gain = gain + 2.0 * shift_value * added
    return (new_factor, new_gain, gram)


def solution(mesh):
    placed = (
        P(None, "gz", None, "gx", None),
        P(None, "gz", None, "gx", None),
        P("gz", "gx", None),
        P(),
        P(),
    )
    return jax.shard_map(
        shards,
        mesh=mesh,
        in_specs=placed,
        out_specs=(P(None, "gz", None, "gx", None), P(None, "gz", None, "gx", None), P()),
        check_vma=False,
    )
```

time: 332 us -> 117 us (0.35)
  blocking collectives: 137 us -> 0 us
  Pallas kernels: 0 us -> 102 us
  starting transfers between devices: 102 us -> 0 us
  waiting for transfers between devices: 55.9 us -> 0 us
  matrix products: 13.4 us -> 0 us
  other arithmetic: 13.5 us -> 2.39 us
  local copies, waits for them, and re-layouts: 5.2 us -> 9.96 us
    psum x1 -> x0, blocking collectives: 115 us -> none  [shards(): gram_total, readout = lax.psum((gram_local, readout_local), ('gx', 'gz'))]
    pallas_call x0 -> x1, Pallas kernels: none -> 102 us  [solve(): pl.pallas_call(functools.partial(step_kernel, sizes), out_shape=(jax.Shap...]
    ppermute x26 -> x0, starting transfers between devices: 88.9 us -> none  [the longest x13 54.9 us: padded_2(): lax.ppermute(head, axis, [((i + 1) % count, i) for i in range(ends)])]
    all_to_all x3 -> x0, waiting for transfers between devices: 33.4 us -> none  [the longest x2 21.9 us: turn_modes(): return lax.all_to_all(turned, 'gz', split_axis=0, concat_axis=1, tiled=True)]
    ppermute x26 -> x0, waiting for transfers between devices: 22.6 us -> none  [the longest x13 11.6 us: padded_2(): lax.ppermute(tail, axis, [(i, (i + 1) % count) for i in range(ends)])]
    all_to_all x1 -> x0, blocking collectives: 22 us -> none  [transform(): lax.all_to_all(flat, 'gz', split_axis=1, concat_axis=0, tiled=True)]
    all_to_all x3 -> x0, starting transfers between devices: 13.4 us -> none  [the longest x2 7.04 us: turn_modes(): return lax.all_to_all(turned, 'gz', split_axis=0, concat_axis=1, tiled=True)]
    dot_general x5 -> x0, matrix products: 13.4 us -> none  [the longest x1 4.4 us: shards(): jnp.einsum('szxy,czjxy->scj', located.astype(jnp.float32), solved, precis...]
  transfers between devices with their start and end apart: 29 -> 0, of which waited for: 26 -> 0; matrix products, arithmetic and copies ran while one was open for 0% -> 0% of each run, Pallas kernels for 0% -> 0%
where the time goes in v2:
time: 117 us
  Pallas kernels  102 us (87%)
  local copies, waits for them, and re-layouts  9.96 us (9%)
  other arithmetic  2.39 us (2%)
  between operations  1.89 us (2%)
    pallas_call x1, Pallas kernels, solve(): pl.pallas_call(functools.partial(step_kernel, sizes), out_shape=(jax.Shap...  102 us
    unnamed x14, local copies, waits for them, and re-layouts  8.34 us

profile of v2, /device:TPU:1, one launch (start us, length us, event | category | flops | bytes accessed | tf_op | source)
XLA Modules:
  0.0 116.6 jit_solution(9430917285324916789)
XLA Ops:
  1.3 0.0 copy-start.4
  1.3 0.6 copy-done.4
  1.9 0.6 fusion
  3.1 1.5 %copy.28 = f32[16,4,256]{2,0,1:T(8,128)} copy(f32[16,4,256]{2,1,0:T(4,128)} %param.10) | data formatting | bytes 131072 | tf_op args[2]
  4.5 2.5 %copy.27 = f32[3,16,4,4,256]{4,1,2,3,0:T(8,128)} copy(f32[3,16,4,4,256]{4,3,2,1,0:T(4,128)} %param.8) | data formatting | bytes 1572864 | tf_op args[0]
  7.0 0.0 copy-start.2
  7.0 102.4 %solve.1 = (f32[3,4,4,16,256]{4,3,2,1,0:T(8,128)}, f32[8,128]{1,0:T(8,128)}) custom-call(f32[1]{0:T(128)} %bitcast.1.shift_ref, s32[4,4]{1,0:T(4,128)} %cells_ref.1, f32[3,4,4,16,256]{4,3,2,1,0:T(8,128)} %bitcast.20, f32[4,16,256]{2,1,0:T(8,128)} %bitcast.21, f32[256,256]{1,0:T(8,128)} %constant.14.clone.table_ref, f32[256,256]{1,0:T(8,128)} %constant.15.clone.scale_ref), custom_call_target="tpu_custom_call" | custom-call | tf_op jit(solution)/shard_map/solve/pallas_call | solution.py:385
  109.4 0.0 copy-start.3
  109.4 0.7 copy-done.3
  110.1 0.6 slice_multiply_fusion
  110.7 0.2 slice_reduce_fusion.3
  110.9 0.0 copy-start
  110.9 0.0 copy-start.1
  110.9 1.4 %slice_bitcast_fusion.3 = (f32[3,16,4,256]{3,1,2,0:T(8,128)S(1)}, f32[3,16,4,256]{3,1,2,0:T(8,128)S(1)}, f32[3,16,4,256]{3,1,2,0:T(8,128)S(1)}, f32[3,16,4,256]{3,1,2,0:T(8,128)S(1)}) fusion(f32[3,16,4,4,256]{4,1,2,3,0:T(8,128)} %bitcast.19), kind=kLoop, calls=%fused_computation.6 | loop fusion | bytes 1572864 | tf_op jit(solution)/shard_map/mul | solution.py:450
  112.3 0.0 copy-done.2
  112.3 0.0 copy-done
  112.4 0.2 copy-done.1
  112.6 1.2 %copy_add_fusion = (f32[3,16,4,4,256]{4,1,2,3,0:T(8,128)S(1)}, f32[3,16,4,4,256]{4,1,2,3,0:T(8,128)S(1)}) fusion(f32[3,16,4,4,256]{4,3,2,1,0:T(4,128)S(1)} %copy-done.2, f32[4]{0:T(128)S(1)} %get-tuple-element.14, f32[3,16,4,256]{3,1,2,0:T(8,128)S(1)} %get-tuple-element.20, f32[4]{0:T(128)S(1)} %get-tuple-element.15, ...), kind=kLoop, calls=%fused_computation | loop fusion | flops 2162688 | bytes 4718660 | tf_op jit(solution)/shard_map/add | solution.py:453
  113.8 1.4 %copy.22 = f32[3,16,4,4,256]{4,3,2,1,0:T(4,128)} copy(f32[3,16,4,4,256]{4,1,2,3,0:T(8,128)S(1)} %get-tuple-element.21) | data formatting | bytes 1572864
  115.2 1.4 %copy.21 = f32[3,16,4,4,256]{4,3,2,1,0:T(4,128)} copy(f32[3,16,4,4,256]{4,1,2,3,0:T(8,128)S(1)} %get-tuple-element.22) | data formatting | bytes 1572864
Async XLA Ops:
  1.3 0.7 copy-start.4
  7.0 105.3 %copy-start.2 = (f32[3,16,4,4,256]{4,3,2,1,0:T(4,128)S(1)}, f32[3,16,4,4,256]{4,3,2,1,0:T(4,128)}, u32[]{:S(2)}) copy-start(f32[3,16,4,4,256]{4,3,2,1,0:T(4,128)} %param.9) | copy-start | bytes 2359300
  109.4 0.7 copy-start.3
  110.9 1.5 %copy-start = (f32[3,16,4,4,256]{4,3,2,1,0:T(4,128)S(1)}, f32[3,16,4,4,256]{4,3,2,1,0:T(4,128)}, u32[]{:S(2)}) copy-start(f32[3,16,4,4,256]{4,3,2,1,0:T(4,128)} %param.8) | copy-start | bytes 2359300
  110.9 1.7 %copy-start.1 = (f32[3,4,4,16,256]{4,3,2,1,0:T(8,128)S(1)}, f32[3,4,4,16,256]{4,3,2,1,0:T(8,128)}, u32[]{:S(2)}) copy-start(f32[3,4,4,16,256]{4,3,2,1,0:T(8,128)} %get-tuple-element.5) | copy-start | bytes 2359300

commit v3 on v2

--- a/solution.py
+++ b/solution.py
@@ -66,7 +66,9 @@
     before_gx = ((gx + count_gx - 1) % count_gx, gz)
     next_gz = (gx, (gz + 1) % count_z)
     before_gz = (gx, (gz + count_z - 1) % count_z)
-    shift = shift_ref[0]
+    shift = jnp.float32(shift_table[0])
+    for entry in range(1, SHIFTS):
+        shift = jnp.where(shift_ref[0] == entry, jnp.float32(shift_table[entry]), shift)
 
     odd = gx % 2
     turn = 1 - 2 * odd
@@ -153,8 +155,8 @@
             )
         return copies
 
-    def keep(level, part, index, block):
-        cell, column = lax.div(index, columns), lax.rem(index, columns)
+    def keep(level, part, cell, column, block):
+        index = cell * columns + column
         fields[level, part, cell + 1, column] = block
         row_sends[level, part, 0, index] = block[span_cells - 1 :]
         row_sends[level, part, 1, index] = block[:1]
@@ -164,11 +166,11 @@
 
     loop(0, stream_cells, invert)
     for part in range(components):
-        def first_guess(index, part=part):
-            cell, column = lax.div(index, columns), lax.rem(index, columns)
-            keep(0, part, index, -factor_ref[part, cell, column] * inverse[cell])
-
-        loop(0, cells, first_guess)
+        def first_guess(cell, part=part):
+            for column in range(columns):
+                keep(0, part, cell, column, -factor_ref[part, cell, column] * inverse[cell])
+
+        loop(0, stream_cells, first_guess)
         if part == 0:
             pl.semaphore_wait(barrier, sum(counts) - 3 + 2)
         for copy in halo_copies(0, part):
@@ -178,107 +180,126 @@
             for copy in halo_copies(level, part):
                 copy.wait()
 
-            def sweep(index, level=level, part=part):
-                cell, column = lax.div(index, columns), lax.rem(index, columns)
-                block = fields[level, part, cell + 1, column]
-                behind = fields[level, part, cell, column] * low(cell)
-                around = behind + fields[level, part, cell + 2, column] * high(cell)
-                around = around + normal_before(block) + normal_after(block)
-                around = around + span_before(block, row_halos[level, part, 0, index])
-                around = around + span_after(block, row_halos[level, part, 1, index])
-                total = viscosity * around + base_ref[cell] * behind - factor_ref[part, cell, column]
-                keep(level + 1, part, index, total * inverse[cell])
-
-            loop(0, cells, sweep)
+            def sweep(cell, level=level, part=part):
+                for column in range(columns):
+                    index = cell * columns + column
+                    block = fields[level, part, cell + 1, column]
+                    behind = fields[level, part, cell, column] * low(cell)
+                    around = behind + fields[level, part, cell + 2, column] * high(cell)
+                    around = around + normal_before(block) + normal_after(block)
+                    around = around + span_before(block, row_halos[level, part, 0, index])
+                    around = around + span_after(block, row_halos[level, part, 1, index])
+                    total = viscosity * around + base_ref[cell] * behind
+                    total = total - factor_ref[part, cell, column]
+                    keep(level + 1, part, cell, column, total * inverse[cell])
+
+            loop(0, stream_cells, sweep)
             for copy in halo_copies(level + 1, part):
                 copy.start()
     for part in range(components):
         for copy in halo_copies(SWEEPS, part):
             copy.wait()
 
-    def diverge(index):
-        cell, column = lax.div(index, columns), lax.rem(index, columns)
+    def spread(step):
+        return count_z // 2 + step // 2 * (1 - 2 * (step % 2))
+
+    def diverge(target):
+        cell, column = mirrored(target % stream_cells), target // stream_cells
+        index = cell * columns + column
         normal = fields[SWEEPS, 1, cell + 1, column]
         span = fields[SWEEPS, 2, cell + 1, column]
         total = 2.0 * (
             fields[SWEEPS, 0, cell + 1, column] - fields[SWEEPS, 0, cell, column] * low(cell)
         )
         total = total + (normal - normal_before(normal))
-        total = total + (span - span_before(span, row_halos[SWEEPS, 2, 0, index]))
-        blocks[column * stream_cells + mirrored(cell)] = -total
-
-    loop(0, cells, diverge)
-
-    def gather_copy(offset):
+        return -(total + (span - span_before(span, row_halos[SWEEPS, 2, 0, index])))
+
+    def gather_copy(step):
+        offset = spread(step)
         device = partner(0, offset)
         return remote(
             blocks.at[device[1]], planes.at[gz], turn_send.at[0, offset], turn_recv.at[0, offset], device
         )
 
-    loop(1, count_z, lambda offset: gather_copy(offset).start())
-    planes[gz] = blocks[gz]
-    loop(1, count_z, lambda offset: gather_copy(offset).wait())
+    def gather_start(step):
+        target = partner(0, spread(step))[1]
+        blocks[target] = diverge(target)
+        gather_copy(step).start()
+
+    loop(1, count_z, gather_start)
+    planes[gz] = diverge(gz)
+    loop(1, count_z, lambda step: gather_copy(step).wait())
     span_total = count_z * span_cells
+    chunks = 4
+    group = count_z // chunks
+    height = span_total // chunks
+    shape = (group, span_cells, normal_cells)
+
+    def mode_copies(level, chunk):
+        part = pl.ds(chunk * group, group)
+        return [
+            remote(
+                modes.at[level, part],
+                beside.at[level, side, part],
+                mode_send.at[level, side, chunk],
+                mode_recv.at[level, side, chunk],
+                device,
+            )
+            for side, device in enumerate((plane_next, plane_before))
+        ]
+
     whole = planes[...].reshape(span_total, normal_cells)
-    spectrum = jnp.dot(
-        table_ref[...], whole, precision=highest, preferred_element_type=jnp.float32
-    ) * scale_ref[...]
-    shape = (count_z, span_cells, normal_cells)
-    rhs[...] = spectrum.reshape(shape)
-    modes[0] = (chebyshev_weights[0] * spectrum).reshape(shape)
-
-    def mode_copies(level):
-        return (
-            remote(
-                modes.at[level], beside.at[level, 0], mode_send.at[level, 0], mode_recv.at[level, 0], plane_next
-            ),
-            remote(
-                modes.at[level], beside.at[level, 1], mode_send.at[level, 1], mode_recv.at[level, 1], plane_before
-            ),
-        )
+    for chunk in range(chunks):
+        lines = slice(chunk * height, (chunk + 1) * height)
+        spectrum = jnp.dot(
+            table_ref[lines, :], whole, precision=highest, preferred_element_type=jnp.float32
+        ) * scale_ref[lines, :]
+        part = slice(chunk * group, (chunk + 1) * group)
+        rhs[part] = spectrum.reshape(shape)
+        modes[0, part] = (chebyshev_weights[0] * spectrum).reshape(shape)
+        for copy in mode_copies(0, chunk):
+            copy.start()
 
     plane_low, plane_high = 4.0 * low(plane_cell), 4.0 * high(plane_cell)
     for level in range(POISSON - 1):
-        for copy in mode_copies(level):
-            copy.start()
-        for copy in mode_copies(level):
-            copy.wait()
         weight = chebyshev_weights[level + 1]
-
-        def smooth(index, level=level, weight=weight):
-            block = modes[level, index]
-            around = plane_low * beside[level, 0, index] + plane_high * beside[level, 1, index]
-            around = around + normal_before(block) + normal_after(block)
-            scale = scale_ref[pl.ds(pl.multiple_of(index * span_cells, span_cells), span_cells), :]
-            modes[level + 1, index] = (1.0 - weight) * block + weight * (rhs[index] + scale * around)
-
-        loop(0, count_z, smooth)
+        for chunk in range(chunks):
+            for copy in mode_copies(level, chunk):
+                copy.wait()
+            for index in range(chunk * group, (chunk + 1) * group):
+                block = modes[level, index]
+                around = plane_low * beside[level, 0, index] + plane_high * beside[level, 1, index]
+                around = around + normal_before(block) + normal_after(block)
+                scale = scale_ref[index * span_cells : (index + 1) * span_cells, :]
+                modes[level + 1, index] = (1.0 - weight) * block + weight * (rhs[index] + scale * around)
+            if level < POISSON - 2:
+                for copy in mode_copies(level + 1, chunk):
+                    copy.start()
     whole = modes[POISSON - 1].reshape(span_total, normal_cells)
     back = jnp.dot(table_ref[...], whole, precision=highest, preferred_element_type=jnp.float32)
-    rhs[...] = back.reshape(shape)
-
-    def scatter_copy(offset):
+    blocks[...] = back.reshape(count_z, span_cells, normal_cells)
+
+    def scatter_copy(step):
+        offset = spread(step)
         device = partner(0, offset)
         return remote(
-            rhs.at[device[1]],
+            blocks.at[device[1]],
             pressure.at[plane_cell, plane_column],
             turn_send.at[1, offset],
             turn_recv.at[1, offset],
             device,
         )
 
-    loop(1, count_z, lambda offset: scatter_copy(offset).start())
-    pressure[plane_cell, plane_column] = rhs[gz]
-    loop(1, count_z, lambda offset: scatter_copy(offset).wait())
-
-    def first_row(index):
-        cell, column = lax.div(index, columns), lax.rem(index, columns)
-        pressure_row[index] = pressure[cell, column][:1]
-
-    loop(0, cells, first_row)
+    loop(1, count_z, lambda step: scatter_copy(step).start())
+    pressure[plane_cell, plane_column] = blocks[gz]
+    loop(1, count_z, lambda step: scatter_copy(step).wait())
+
+    for cell in range(stream_cells):
+        for column in range(columns):
+            pressure_row[cell * columns + column] = pressure[cell, column][:1]
     copies = (
-        remote(pressure.at[0], pressure.at[stream_cells], mode_send.at[POISSON - 1, 0], mode_recv.at[POISSON - 1, 0], before_gx),
-        remote(pressure_row, pressure_halo, mode_send.at[POISSON - 1, 1], mode_recv.at[POISSON - 1, 1], before_gz),
+        remote(pressure.at[0], pressure.at[stream_cells], mode_send.at[POISSON - 1, 0, 0], mode_recv.at[POISSON - 1, 0, 0], before_gx),
+        remote(pressure_row, pressure_halo, mode_send.at[POISSON - 1, 1, 0], mode_recv.at[POISSON - 1, 1, 0], before_gz),
     )
     for copy in copies:
         copy.start()
@@ -411,8 +432,8 @@
             dma((SWEEPS + 1, components, 4)),
             dma((2, count_z)),
             dma((2, count_z)),
-            dma((POISSON, 2)),
-            dma((POISSON, 2)),
+            dma((POISSON, 2, 4)),
+            dma((POISSON, 2, 4)),
             dma((sum(sizes),)),
             dma((sum(sizes),)),
         ],
@@ -436,7 +457,7 @@
     shift_values = jnp.asarray(shift_table, jnp.float32)
     shift_value = jnp.sum(jnp.where(jnp.arange(SHIFTS) == shift_index[0], shift_values, 0.0))
     solved, tile = solve(
-        shift_value[None],
+        shift_index,
         sensor_cells,
         jnp.transpose(factor, (0, 3, 2, 1, 4)),
         jnp.transpose(base_flow, (1, 0, 2)),

time: 117 us -> 103 us (0.88)
  Pallas kernels: 102 us -> 87.7 us
    pallas_call x1, Pallas kernels: 102 us -> 87.7 us  [solve(): pl.pallas_call(functools.partial(step_kernel, sizes), out_shape=(jax.Shap...]
where the time goes in v3:
time: 103 us; the launch traced here: 102 us
  Pallas kernels  87.7 us (85%)
  local copies, waits for them, and re-layouts  9.96 us (10%)
  other arithmetic  2.41 us (2%)
  between operations  1.99 us (2%)
    pallas_call x1, Pallas kernels, solve(): pl.pallas_call(functools.partial(step_kernel, sizes), out_shape=(jax.Shap...  87.7 us
    unnamed x14, local copies, waits for them, and re-layouts  8.34 us

profile of v3, /device:TPU:1, one launch (start us, length us, event | category | flops | bytes accessed | tf_op | source)
XLA Modules:
  0.0 102.0 jit_solution(2411422958436248258)
XLA Ops:
  1.3 0.0 copy-start.4
  1.3 0.6 copy-done.4
  1.9 0.6 fusion
  3.2 1.5 %copy.28 = f32[16,4,256]{2,0,1:T(8,128)} copy(f32[16,4,256]{2,1,0:T(4,128)} %param.10) | data formatting | bytes 131072 | tf_op args[2]
  4.7 2.5 %copy.27 = f32[3,16,4,4,256]{4,1,2,3,0:T(8,128)} copy(f32[3,16,4,4,256]{4,3,2,1,0:T(4,128)} %param.8) | data formatting | bytes 1572864 | tf_op args[0]
  7.1 0.0 copy-start.2
  7.1 87.7 %solve.1 = (f32[3,4,4,16,256]{4,3,2,1,0:T(8,128)}, f32[8,128]{1,0:T(8,128)}) custom-call(s32[1]{0:T(128)} %copy.29.shift_ref, s32[4,4]{1,0:T(4,128)} %cells_ref.1, f32[3,4,4,16,256]{4,3,2,1,0:T(8,128)} %bitcast.19, f32[4,16,256]{2,1,0:T(8,128)} %bitcast.20, f32[256,256]{1,0:T(8,128)} %constant.14.clone.table_ref, f32[256,256]{1,0:T(8,128)} %constant.15.clone.scale_ref), custom_call_target="tpu_custom_call" | custom-call | tf_op jit(solution)/shard_map/solve/pallas_call | solution.py:406
  94.8 0.0 copy-start.3
  94.8 0.7 copy-done.3
  95.5 0.6 slice_multiply_fusion
  96.1 0.2 slice_reduce_fusion.3
  96.3 0.0 copy-start
  96.3 0.0 copy-start.1
  96.3 1.4 %slice_bitcast_fusion.3 = (f32[3,16,4,256]{3,1,2,0:T(8,128)S(1)}, f32[3,16,4,256]{3,1,2,0:T(8,128)S(1)}, f32[3,16,4,256]{3,1,2,0:T(8,128)S(1)}, f32[3,16,4,256]{3,1,2,0:T(8,128)S(1)}) fusion(f32[3,16,4,4,256]{4,1,2,3,0:T(8,128)} %bitcast.18), kind=kLoop, calls=%fused_computation.6 | loop fusion | bytes 1572864 | tf_op jit(solution)/shard_map/mul | solution.py:471
  97.7 0.0 copy-done.2
  97.8 0.0 copy-done
  97.8 0.2 copy-done.1
  98.0 1.2 %copy_add_fusion = (f32[3,16,4,4,256]{4,1,2,3,0:T(8,128)S(1)}, f32[3,16,4,4,256]{4,1,2,3,0:T(8,128)S(1)}) fusion(f32[3,16,4,4,256]{4,3,2,1,0:T(4,128)S(1)} %copy-done.2, f32[4]{0:T(128)S(1)} %get-tuple-element.14, f32[3,16,4,256]{3,1,2,0:T(8,128)S(1)} %get-tuple-element.20, f32[4]{0:T(128)S(1)} %get-tuple-element.15, ...), kind=kLoop, calls=%fused_computation | loop fusion | flops 2162688 | bytes 4718660 | tf_op jit(solution)/shard_map/add | solution.py:474
  99.3 1.4 %copy.22 = f32[3,16,4,4,256]{4,3,2,1,0:T(4,128)} copy(f32[3,16,4,4,256]{4,1,2,3,0:T(8,128)S(1)} %get-tuple-element.21) | data formatting | bytes 1572864
  100.7 1.4 %copy.21 = f32[3,16,4,4,256]{4,3,2,1,0:T(4,128)} copy(f32[3,16,4,4,256]{4,1,2,3,0:T(8,128)S(1)} %get-tuple-element.22) | data formatting | bytes 1572864
Async XLA Ops:
  1.3 0.7 copy-start.4
  7.1 90.6 %copy-start.2 = (f32[3,16,4,4,256]{4,3,2,1,0:T(4,128)S(1)}, f32[3,16,4,4,256]{4,3,2,1,0:T(4,128)}, u32[]{:S(2)}) copy-start(f32[3,16,4,4,256]{4,3,2,1,0:T(4,128)} %param.9) | copy-start | bytes 2359300
  94.8 0.7 copy-start.3
  96.3 1.5 %copy-start = (f32[3,16,4,4,256]{4,3,2,1,0:T(4,128)S(1)}, f32[3,16,4,4,256]{4,3,2,1,0:T(4,128)}, u32[]{:S(2)}) copy-start(f32[3,16,4,4,256]{4,3,2,1,0:T(4,128)} %param.8) | copy-start | bytes 2359300
  96.3 1.7 %copy-start.1 = (f32[3,4,4,16,256]{4,3,2,1,0:T(8,128)S(1)}, f32[3,4,4,16,256]{4,3,2,1,0:T(8,128)}, u32[]{:S(2)}) copy-start(f32[3,4,4,16,256]{4,3,2,1,0:T(8,128)} %get-tuple-element.5) | copy-start | bytes 2359300

commit v4 on v3

--- a/solution.py
+++ b/solution.py
@@ -24,12 +24,18 @@
     sizes,
     shift_ref,
     cells_ref,
+    given_factor,
+    gain_ref,
+    given_base,
+    table_ref,
+    scale_ref,
+    new_factor_ref,
+    new_gain_ref,
+    gram_ref,
     factor_ref,
     base_ref,
-    table_ref,
-    scale_ref,
     solved_ref,
-    out_ref,
+    natural,
     fields,
     inverse,
     row_sends,
@@ -57,7 +63,7 @@
 ):
     count_z, count_x, count_y = sizes
     count_gx = count_x * count_y
-    components, stream_cells, columns, span_cells, normal_cells = factor_ref.shape
+    components, span_cells, columns, stream_cells, normal_cells = given_factor.shape
     last_cell = stream_cells - 1
     cells = stream_cells * columns
     gx, gz = lax.axis_index("gx"), lax.axis_index("gz")
@@ -161,16 +167,15 @@
         row_sends[level, part, 0, index] = block[span_cells - 1 :]
         row_sends[level, part, 1, index] = block[:1]
 
-    def invert(cell):
+    for cell in range(stream_cells):
+        base_ref[cell] = given_base[:, cell, :]
         inverse[cell] = 1.0 / (shift + 6.0 * viscosity + base_ref[cell])
-
-    loop(0, stream_cells, invert)
     for part in range(components):
-        def first_guess(cell, part=part):
+        for cell in range(stream_cells):
             for column in range(columns):
-                keep(0, part, cell, column, -factor_ref[part, cell, column] * inverse[cell])
-
-        loop(0, stream_cells, first_guess)
+                block = given_factor[part, :, column, cell, :]
+                factor_ref[part, cell, column] = block
+                keep(0, part, cell, column, -block * inverse[cell])
         if part == 0:
             pl.semaphore_wait(barrier, sum(counts) - 3 + 2)
         for copy in halo_copies(0, part):
@@ -370,6 +375,13 @@
             )
 
         loop(1, counts[stage], lambda offset, sum_copy=sum_copy: sum_copy(offset).start())
+        if stage == 0:
+            for part in range(components):
+                for cell in range(stream_cells):
+                    for column in range(columns):
+                        block = solved_ref[part, cell, column] * (2.0 * shift)
+                        natural[part, :, column, cell, :] = block
+                        new_factor_ref[part, :, column, cell, :] = factor_ref[part, cell, column] + block
         slots[places[stage]] = mid[stage]
         loop(1, counts[stage], lambda offset, sum_copy=sum_copy: sum_copy(offset).wait())
         total = slots[0]
@@ -378,7 +390,21 @@
         if stage < 2:
             mid[stage + 1] = total
         else:
-            out_ref[...] = total
+            gram_ref[...] = total[:columns, :columns] * (1.0 / (components * cells * normal_cells * span_cells * count_z * count_gx / columns))
+            readout = [
+                [total[columns + i : columns + i + 1, j : j + 1] for j in range(columns)] for i in range(columns)
+            ]
+
+            def gain(span):
+                for part in range(components):
+                    steps = [natural[part, span, j] for j in range(columns)]
+                    for i in range(columns):
+                        value = gain_ref[part, span, i]
+                        for j in range(columns):
+                            value = value + steps[j] * readout[i][j]
+                        new_gain_ref[part, span, i] = value
+
+            loop(0, span_cells, gain)
 
 
 def hartley_table(span_total):
@@ -393,25 +419,31 @@
     return np.repeat((1.0 / diagonal).astype(np.float32)[:, None], normal_cells, axis=1)
 
 
-def solve(shift, sensor_cells, turned_factor, turned_base, sizes):
+def solve(factor, gain, base_flow, shift_index, sensor_cells, sizes):
     count_z, count_x, count_y = sizes
-    components, stream_cells, columns, span_cells, normal_cells = turned_factor.shape
+    components, span_cells, columns, stream_cells, normal_cells = factor.shape
     cells = stream_cells * columns
     span_total = count_z * span_cells
     vmem = pl.BlockSpec(memory_space=pltpu.VMEM)
     smem = pl.BlockSpec(memory_space=pltpu.SMEM)
     f32 = jnp.float32
     group = (count_z, span_cells, normal_cells)
+    turned = (components, stream_cells, columns, span_cells, normal_cells)
     dma = pltpu.SemaphoreType.DMA
     return pl.pallas_call(
         functools.partial(step_kernel, sizes),
         out_shape=(
-            jax.ShapeDtypeStruct(turned_factor.shape, f32),
-            jax.ShapeDtypeStruct((8, 128), f32),
+            jax.ShapeDtypeStruct(factor.shape, f32),
+            jax.ShapeDtypeStruct(gain.shape, f32),
+            jax.ShapeDtypeStruct((columns, columns), f32),
         ),
-        in_specs=[smem, smem, vmem, vmem, vmem, vmem],
-        out_specs=(vmem, vmem),
+        in_specs=[smem, smem, vmem, vmem, vmem, vmem, vmem],
+        out_specs=(vmem, vmem, vmem),
         scratch_shapes=[
+            pltpu.VMEM(turned, f32),
+            pltpu.VMEM((stream_cells, span_cells, normal_cells), f32),
+            pltpu.VMEM(turned, f32),
+            pltpu.VMEM(factor.shape, f32),
             pltpu.VMEM((SWEEPS + 1, components, stream_cells + 2, columns, span_cells, normal_cells), f32),
             pltpu.VMEM((stream_cells, span_cells, normal_cells), f32),
             pltpu.VMEM((SWEEPS + 1, components, 2, cells, 1, normal_cells), f32),
@@ -440,39 +472,21 @@
         compiler_params=pltpu.CompilerParams(collective_id=0, has_side_effects=True),
         name="solve",
     )(
-        shift,
+        shift_index,
         sensor_cells,
-        turned_factor,
-        turned_base,
+        factor,
+        gain,
+        base_flow,
         jnp.asarray(hartley_table(span_total)),
         jnp.asarray(mode_scale(span_total, normal_cells)),
     )
 
 
 def shards(factor, gain, base_flow, shift_index, sensor_cells):
-    components, span_cells, columns, stream_cells, normal_cells = factor.shape
     count_gx, count_z = lax.axis_size("gx"), lax.axis_size("gz")
     count_x = 4 if count_gx % 4 == 0 else count_gx
     sizes = (count_z, count_x, count_gx // count_x)
-    shift_values = jnp.asarray(shift_table, jnp.float32)
-    shift_value = jnp.sum(jnp.where(jnp.arange(SHIFTS) == shift_index[0], shift_values, 0.0))
-    solved, tile = solve(
-        shift_index,
-        sensor_cells,
-        jnp.transpose(factor, (0, 3, 2, 1, 4)),
-        jnp.transpose(base_flow, (1, 0, 2)),
-        sizes,
-    )
-    solved = jnp.transpose(solved, (0, 3, 2, 1, 4))
-    gram_total, readout = tile[:columns, :columns], tile[columns : 2 * columns, :columns]
-    new_factor = factor + 2.0 * shift_value * solved
-    total_cells = components * stream_cells * count_gx * normal_cells * span_cells * count_z
-    gram = gram_total / float(total_cells)
-    added = solved[:, :, 0:1] * readout[None, None, :, 0, None, None]
-    for column in range(1, columns):
-        added = added + solved[:, :, column : column + 1] * readout[None, None, :, column, None, None]
-    new_gain = gain + 2.0 * shift_value * added
-    return (new_factor, new_gain, gram)
+    return solve(factor, gain, base_flow, shift_index, sensor_cells, sizes)
 
 
 def solution(mesh):

time: 103 us -> 95.3 us (0.925)
  local copies, waits for them, and re-layouts: 9.96 us -> 3.69 us
  other arithmetic: 2.41 us -> 0 us
  Pallas kernels: 87.7 us -> 89.9 us
    unnamed x14 -> x7, local copies, waits for them, and re-layouts: 8.34 us -> 3.69 us
    pallas_call x1, Pallas kernels: 87.7 us -> 89.9 us  [solve(): pl.pallas_call(functools.partial(step_kernel, sizes), out_shape=(jax.Shap...]
    mul x1 -> x0, local copies, waits for them, and re-layouts: 1.41 us -> none  [shards(): added = solved[:, :, 0:1] * readout[None, None, :, 0, None, None]]
    add x1 -> x0, other arithmetic: 1.24 us -> none  [shards(): new_gain = gain + 2.0 * shift_value * added]
where the time goes in v4:
time: 95.3 us; the launch traced here: 94.8 us
  Pallas kernels  89.9 us (94%)
  local copies, waits for them, and re-layouts  3.69 us (4%)
  between operations  1.3 us (1%)
    pallas_call x1, Pallas kernels, solve(): pl.pallas_call(functools.partial(step_kernel, sizes), out_shape=(jax.Shap...  89.9 us
    unnamed x7, local copies, waits for them, and re-layouts  3.69 us

profile of v4, /device:TPU:1, one launch (start us, length us, event | category | flops | bytes accessed | tf_op | source)
XLA Modules:
  0.0 94.8 jit_solution(467527877449550569)
XLA Ops:
  1.3 89.9 %solve.1 = (f32[3,16,4,4,256]{4,3,2,1,0:T(4,128)}, f32[3,16,4,4,256]{4,3,2,1,0:T(4,128)}, f32[4,4]{1,0:T(4,128)}) custom-call(s32[1]{0:T(128)S(6)} %copy.13.shift_ref, s32[4,4]{1,0:T(4,128)} %cells_ref.1, f32[3,16,4,4,256]{4,3,2,1,0:T(4,128)} %given_factor.1, f32[3,16,4,4,256]{4,3,2,1,0:T(4,128)} %gain_ref.1, f32[16,4,256]{2,1,0:T(4,128)} %given_base.1, ...), custom_call_target="tpu_custom_call" | custom-call | tf_op jit(solution)/shard_map/solve/pallas_call | solution.py:433
  91.1 0.0 copy-start
  91.2 2.2 %copy.14 = f32[3,16,4,4,256]{4,3,2,1,0:T(4,128)} copy(f32[3,16,4,4,256]{4,3,2,1,0:T(4,128)} %get-tuple-element.6) | data formatting | bytes 1572864
  93.4 0.0 copy-done
  93.4 0.0 copy-start.1
  93.4 0.9 copy.15
  94.3 0.0 copy-done.1
  94.3 0.6 copy.16
Async XLA Ops:
  91.1 2.2 %copy-start = (f32[3,16,4,4,256]{4,3,2,1,0:T(4,128)S(1)}, f32[3,16,4,4,256]{4,3,2,1,0:T(4,128)}, u32[]{:S(2)}) copy-start(f32[3,16,4,4,256]{4,3,2,1,0:T(4,128)} %get-tuple-element.7) | copy-start | bytes 2359300
  93.4 0.9 copy-start.1

commit v5 on v4

--- a/solution.py
+++ b/solution.py
@@ -29,13 +29,12 @@
     given_base,
     table_ref,
     scale_ref,
-    new_factor_ref,
+    natural,
     new_gain_ref,
     gram_ref,
     factor_ref,
     base_ref,
     solved_ref,
-    natural,
     fields,
     inverse,
     row_sends,
@@ -176,12 +175,13 @@
                 block = given_factor[part, :, column, cell, :]
                 factor_ref[part, cell, column] = block
                 keep(0, part, cell, column, -block * inverse[cell])
-        if part == 0:
-            pl.semaphore_wait(barrier, sum(counts) - 3 + 2)
+    pl.semaphore_wait(barrier, sum(counts) - 3 + 2)
+    order = (0, 2, 1)
+    for part in order:
         for copy in halo_copies(0, part):
             copy.start()
     for level in range(SWEEPS):
-        for part in range(components):
+        for part in order:
             for copy in halo_copies(level, part):
                 copy.wait()
 
@@ -281,11 +281,8 @@
                 for copy in mode_copies(level + 1, chunk):
                     copy.start()
     whole = modes[POISSON - 1].reshape(span_total, normal_cells)
-    back = jnp.dot(table_ref[...], whole, precision=highest, preferred_element_type=jnp.float32)
-    blocks[...] = back.reshape(count_z, span_cells, normal_cells)
-
-    def scatter_copy(step):
-        offset = spread(step)
+
+    def scatter_copy(offset):
         device = partner(0, offset)
         return remote(
             blocks.at[device[1]],
@@ -295,9 +292,22 @@
             device,
         )
 
-    loop(1, count_z, lambda step: scatter_copy(step).start())
+    for chunk in range(chunks):
+        chosen = (gz // group + chunks // 2 + chunk) % chunks
+        lines = pl.ds(pl.multiple_of(chosen * height, height), height)
+        back = jnp.dot(table_ref[lines, :], whole, precision=highest, preferred_element_type=jnp.float32)
+        blocks[pl.ds(chosen * group, group)] = back.reshape(shape)
+
+        def scatter_start(member, chosen=chosen):
+            target = chosen * group + member
+
+            @pl.when(target != gz)
+            def _():
+                scatter_copy((target + count_z - gz) % count_z).start()
+
+        loop(0, group, scatter_start)
     pressure[plane_cell, plane_column] = blocks[gz]
-    loop(1, count_z, lambda step: scatter_copy(step).wait())
+    loop(1, count_z, lambda offset: scatter_copy(offset).wait())
 
     for cell in range(stream_cells):
         for column in range(columns):
@@ -339,12 +349,11 @@
 
     zero = jnp.zeros((8, half), jnp.float32)
     sums = lax.fori_loop(0, stream_cells, finish, (zero,) * len(pairs))
-    tile_rows = lax.broadcasted_iota(jnp.int32, (8, 128), 0)
-    tile_lanes = lax.broadcasted_iota(jnp.int32, (8, 128), 1)
-    tile = jnp.zeros((8, 128), jnp.float32)
+    tile_lanes = lax.broadcasted_iota(jnp.int32, (1, 128), 1)
+    tile = jnp.zeros((1, 128), jnp.float32)
 
     def put(tile, row, lane, value):
-        return jnp.where((tile_rows == row) & (tile_lanes == lane), value, tile)
+        return jnp.where(tile_lanes == row * columns + lane, value, tile)
 
     for total, (i, j) in zip(sums, pairs):
         value = jnp.sum(jnp.sum(total, axis=1, keepdims=True), axis=0, keepdims=True)
@@ -381,7 +390,6 @@
                     for column in range(columns):
                         block = solved_ref[part, cell, column] * (2.0 * shift)
                         natural[part, :, column, cell, :] = block
-                        new_factor_ref[part, :, column, cell, :] = factor_ref[part, cell, column] + block
         slots[places[stage]] = mid[stage]
         loop(1, counts[stage], lambda offset, sum_copy=sum_copy: sum_copy(offset).wait())
         total = slots[0]
@@ -390,10 +398,19 @@
         if stage < 2:
             mid[stage + 1] = total
         else:
-            gram_ref[...] = total[:columns, :columns] * (1.0 / (components * cells * normal_cells * span_cells * count_z * count_gx / columns))
-            readout = [
-                [total[columns + i : columns + i + 1, j : j + 1] for j in range(columns)] for i in range(columns)
-            ]
+            def entry(row, lane):
+                place = row * columns + lane
+                return total[:, place : place + 1]
+
+            gram_rows = lax.broadcasted_iota(jnp.int32, (columns, columns), 0)
+            gram_lanes = lax.broadcasted_iota(jnp.int32, (columns, columns), 1)
+            gram = jnp.zeros((columns, columns), jnp.float32)
+            for i in range(columns):
+                for j in range(columns):
+                    gram = jnp.where((gram_rows == i) & (gram_lanes == j), entry(i, j), gram)
+            all_cells = components * stream_cells * count_gx * normal_cells * span_cells * count_z
+            gram_ref[...] = gram * (1.0 / all_cells)
+            readout = [[entry(columns + i, j) for j in range(columns)] for i in range(columns)]
 
             def gain(span):
                 for part in range(components):
@@ -443,7 +460,6 @@
             pltpu.VMEM(turned, f32),
             pltpu.VMEM((stream_cells, span_cells, normal_cells), f32),
             pltpu.VMEM(turned, f32),
-            pltpu.VMEM(factor.shape, f32),
             pltpu.VMEM((SWEEPS + 1, components, stream_cells + 2, columns, span_cells, normal_cells), f32),
             pltpu.VMEM((stream_cells, span_cells, normal_cells), f32),
             pltpu.VMEM((SWEEPS + 1, components, 2, cells, 1, normal_cells), f32),
@@ -457,9 +473,9 @@
             pltpu.VMEM((cells, 1, normal_cells), f32),
             pltpu.VMEM((cells, 1, normal_cells), f32),
         ]
-        + [pltpu.VMEM((size, 8, 128), f32) for size in sizes]
+        + [pltpu.VMEM((size, 1, 128), f32) for size in sizes]
         + [
-            pltpu.VMEM((3, 8, 128), f32),
+            pltpu.VMEM((3, 1, 128), f32),
             dma((SWEEPS + 1, components, 4)),
             dma((SWEEPS + 1, components, 4)),
             dma((2, count_z)),
@@ -486,7 +502,8 @@
     count_gx, count_z = lax.axis_size("gx"), lax.axis_size("gz")
     count_x = 4 if count_gx % 4 == 0 else count_gx
     sizes = (count_z, count_x, count_gx // count_x)
-    return solve(factor, gain, base_flow, shift_index, sensor_cells, sizes)
+    step, new_gain, gram = solve(factor, gain, base_flow, shift_index, sensor_cells, sizes)
+    return (factor + step, new_gain, gram)
 
 
 def solution(mesh):

time: 95.3 us -> 94 us (0.986)
  other arithmetic: 0 us -> 2.34 us
  local copies, waits for them, and re-layouts: 3.69 us -> 1.47 us
  Pallas kernels: 89.9 us -> 87.9 us
    add x0 -> x1, other arithmetic: none -> 2.34 us  [shards(): return (factor + step, new_gain, gram)]
    unnamed x7 -> x8, local copies, waits for them, and re-layouts: 3.69 us -> 1.47 us
    pallas_call x1, Pallas kernels: 89.9 us -> 87.9 us  [solve(): pl.pallas_call(functools.partial(step_kernel, sizes), out_shape=(jax.Shap...]
where the time goes in v5:
time: 94 us; the launch traced here: 93 us
  Pallas kernels  87.9 us (94%)
  other arithmetic  2.34 us (2%)
  local copies, waits for them, and re-layouts  1.47 us (2%)
  between operations  1.31 us (1%)
    pallas_call x1, Pallas kernels, solve(): pl.pallas_call(functools.partial(step_kernel, sizes), out_shape=(jax.Shap...  87.9 us
    add x1, other arithmetic, shards(): return (factor + step, new_gain, gram)  2.34 us

profile of v5, /device:TPU:1, one launch (start us, length us, event | category | flops | bytes accessed | tf_op | source)
XLA Modules:
  0.0 93.0 jit_solution(5527124928692540914)
XLA Ops:
  1.3 0.0 copy-start
  1.3 87.9 %solve.1 = (f32[3,16,4,4,256]{4,3,2,1,0:T(4,128)}, f32[3,16,4,4,256]{4,3,2,1,0:T(4,128)}, f32[4,4]{1,0:T(4,128)}) custom-call(s32[1]{0:T(128)S(6)} %copy.12.shift_ref, s32[4,4]{1,0:T(4,128)} %cells_ref.1, f32[3,16,4,4,256]{4,3,2,1,0:T(4,128)} %given_factor.1, f32[3,16,4,4,256]{4,3,2,1,0:T(4,128)} %gain_ref.1, f32[16,4,256]{2,1,0:T(4,128)} %given_base.1, ...), custom_call_target="tpu_custom_call" | custom-call | tf_op jit(solution)/shard_map/solve/pallas_call | solution.py:450
  89.2 0.0 copy-done
  89.2 0.0 copy-start.1
  89.2 2.3 %add.3 = f32[3,16,4,4,256]{4,3,2,1,0:T(4,128)} add(f32[3,16,4,4,256]{4,3,2,1,0:T(4,128)S(1)} %copy-done, f32[3,16,4,4,256]{4,3,2,1,0:T(4,128)} %get-tuple-element.6) | non-fusion elementwise | flops 196608 | bytes 2359296 | tf_op jit(solution)/shard_map/add | solution.py:506
  91.6 0.0 copy-done.1
  91.6 0.0 copy-start.2
  91.6 0.9 copy.13
  92.4 0.0 copy-done.2
  92.4 0.6 copy.14
Async XLA Ops:
  1.3 87.9 %copy-start = (f32[3,16,4,4,256]{4,3,2,1,0:T(4,128)S(1)}, f32[3,16,4,4,256]{4,3,2,1,0:T(4,128)}, u32[]{:S(2)}) copy-start(f32[3,16,4,4,256]{4,3,2,1,0:T(4,128)} %given_factor.1) | copy-start | bytes 2359300
  89.2 2.4 %copy-start.1 = (f32[3,16,4,4,256]{4,3,2,1,0:T(4,128)S(1)}, f32[3,16,4,4,256]{4,3,2,1,0:T(4,128)}, u32[]{:S(2)}) copy-start(f32[3,16,4,4,256]{4,3,2,1,0:T(4,128)} %get-tuple-element.13) | copy-start | bytes 2359300
  91.6 0.9 copy-start.2

commit v6 on v5

--- a/solution.py
+++ b/solution.py
@@ -25,16 +25,20 @@
     shift_ref,
     cells_ref,
     given_factor,
-    gain_ref,
+    far_gain,
     given_base,
-    table_ref,
-    scale_ref,
+    far_table,
+    far_scale,
     natural,
     new_gain_ref,
     gram_ref,
     factor_ref,
     base_ref,
     solved_ref,
+    gain_ref,
+    table_ref,
+    scale_ref,
+    near,
     fields,
     inverse,
     row_sends,
@@ -118,6 +122,14 @@
 
         lax.fori_loop(first, end, run, 0)
 
+    loads = [
+        pltpu.make_async_copy(src, dst, near.at[place])
+        for place, (src, dst) in enumerate(
+            ((far_table, table_ref), (far_scale, scale_ref), (far_gain, gain_ref))
+        )
+    ]
+    for load in loads:
+        load.start()
     counts = (count_z, count_x, count_y)
     barrier = pltpu.get_barrier_semaphore()
 
@@ -253,6 +265,8 @@
             for side, device in enumerate((plane_next, plane_before))
         ]
 
+    loads[0].wait()
+    loads[1].wait()
     whole = planes[...].reshape(span_total, normal_cells)
     for chunk in range(chunks):
         lines = slice(chunk * height, (chunk + 1) * height)
@@ -412,6 +426,8 @@
             gram_ref[...] = gram * (1.0 / all_cells)
             readout = [[entry(columns + i, j) for j in range(columns)] for i in range(columns)]
 
+            loads[2].wait()
+
             def gain(span):
                 for part in range(components):
                     steps = [natural[part, span, j] for j in range(columns)]
@@ -443,6 +459,7 @@
     span_total = count_z * span_cells
     vmem = pl.BlockSpec(memory_space=pltpu.VMEM)
     smem = pl.BlockSpec(memory_space=pltpu.SMEM)
+    far = pl.BlockSpec(memory_space=pl.ANY)
     f32 = jnp.float32
     group = (count_z, span_cells, normal_cells)
     turned = (components, stream_cells, columns, span_cells, normal_cells)
@@ -454,12 +471,16 @@
             jax.ShapeDtypeStruct(gain.shape, f32),
             jax.ShapeDtypeStruct((columns, columns), f32),
         ),
-        in_specs=[smem, smem, vmem, vmem, vmem, vmem, vmem],
+        in_specs=[smem, smem, vmem, far, vmem, far, far],
         out_specs=(vmem, vmem, vmem),
         scratch_shapes=[
             pltpu.VMEM(turned, f32),
             pltpu.VMEM((stream_cells, span_cells, normal_cells), f32),
             pltpu.VMEM(turned, f32),
+            pltpu.VMEM(gain.shape, f32),
+            pltpu.VMEM((span_total, span_total), f32),
+            pltpu.VMEM((span_total, normal_cells), f32),
+            dma((3,)),
             pltpu.VMEM((SWEEPS + 1, components, stream_cells + 2, columns, span_cells, normal_cells), f32),
             pltpu.VMEM((stream_cells, span_cells, normal_cells), f32),
             pltpu.VMEM((SWEEPS + 1, components, 2, cells, 1, normal_cells), f32),

time: 94 us -> 93.7 us (level)
  no operation moved by 1% of the time
where the time goes in v6:
time: 93.7 us; the launch traced here: 92.7 us
  Pallas kernels  87.5 us (93%)
  other arithmetic  2.34 us (2%)
  local copies, waits for them, and re-layouts  1.47 us (2%)
  between operations  1.31 us (1%)
    pallas_call x1, Pallas kernels, solve(): pl.pallas_call(functools.partial(step_kernel, sizes), out_shape=(jax.Shap...  87.5 us
    add x1, other arithmetic, shards(): return (factor + step, new_gain, gram)  2.34 us

profile of v6, /device:TPU:1, one launch (start us, length us, event | category | flops | bytes accessed | tf_op | source)
XLA Modules:
  0.0 92.7 jit_solution(10069809176187225849)
XLA Ops:
  1.3 0.0 copy-start
  1.3 87.5 %solve.1 = (f32[3,16,4,4,256]{4,3,2,1,0:T(4,128)}, f32[3,16,4,4,256]{4,3,2,1,0:T(4,128)}, f32[4,4]{1,0:T(4,128)}) custom-call(s32[1]{0:T(128)S(6)} %copy.12.shift_ref, s32[4,4]{1,0:T(4,128)} %cells_ref.1, f32[3,16,4,4,256]{4,3,2,1,0:T(4,128)} %given_factor.1, f32[3,16,4,4,256]{4,3,2,1,0:T(4,128)} %far_gain.1, f32[16,4,256]{2,1,0:T(4,128)} %given_base.1, ...), custom_call_target="tpu_custom_call" | custom-call | tf_op jit(solution)/shard_map/solve/pallas_call | solution.py:467
  88.8 0.0 copy-done
  88.9 0.0 copy-start.1
  88.9 2.3 %add.3 = f32[3,16,4,4,256]{4,3,2,1,0:T(4,128)} add(f32[3,16,4,4,256]{4,3,2,1,0:T(4,128)S(1)} %copy-done, f32[3,16,4,4,256]{4,3,2,1,0:T(4,128)} %get-tuple-element.6) | non-fusion elementwise | flops 196608 | bytes 2359296 | tf_op jit(solution)/shard_map/add | solution.py:527
  91.2 0.0 copy-done.1
  91.2 0.0 copy-start.2
  91.2 0.9 copy.13
  92.1 0.0 copy-done.2
  92.1 0.6 copy.14
Async XLA Ops:
  1.3 87.6 %copy-start = (f32[3,16,4,4,256]{4,3,2,1,0:T(4,128)S(1)}, f32[3,16,4,4,256]{4,3,2,1,0:T(4,128)}, u32[]{:S(2)}) copy-start(f32[3,16,4,4,256]{4,3,2,1,0:T(4,128)} %given_factor.1) | copy-start | bytes 2359300
  88.9 2.4 %copy-start.1 = (f32[3,16,4,4,256]{4,3,2,1,0:T(4,128)S(1)}, f32[3,16,4,4,256]{4,3,2,1,0:T(4,128)}, u32[]{:S(2)}) copy-start(f32[3,16,4,4,256]{4,3,2,1,0:T(4,128)} %get-tuple-element.13) | copy-start | bytes 2359300
  91.2 0.9 copy-start.2
